TPU v7x, 32 devices: a whole 2x2x4 slice. The times are simulated.
32 devices in a mesh: wide: 8 (over z, y), mp: 4 (over x, core).
Axes of the slice: x: 2, y: 2, z: 4, core: 2. Of those that a mesh axis runs over, the one named last changes fastest.
Arguments:
- clip_feats: bfloat16 [1024, 768], P('wide'), may hold values from -6 to 6
- teacher_audio: bfloat16 [1024, 512], P('wide'), may hold values from -16 to 16
- teacher_text: bfloat16 [1024, 512], P(('wide', 'mp')), may hold values from -16 to 16
- w_first: bfloat16 [768, 512], P(None, 'mp'), may hold values from -0.21875 to 0.21875
- w_second: bfloat16 [512, 512], P('mp'), may hold values from -0.25 to 0.25
- pairing: int32 [1024], P('wide'), may hold values from 0 to 1023
Outputs:
- loss: float32 [], replicated
- grad_first: float32 [768, 512], P(None, 'mp')
- grad_second: float32 [512, 512], P('mp')
All inputs are finite; a program needn't handle non-finite values.
Results may differ from a plain program's by a relative error of at most 0.0052.
Values may be sent and summed in bfloat16 or wider, within the bound.
No kernel may reach another device: no remote copies, remote signals or barrier semaphores. Data moves between devices by JAX's collectives and lax.ppermute only.
A program may use at most 64 MiB of HBM per device.

v0:
```python
import jax
import jax.numpy as jnp
from jax import lax
from jax.experimental import pallas as pl
from jax.experimental.pallas import tpu as pltpu
from jax.sharding import PartitionSpec as P

teacher_scale = 14.0
student_scale = 64.0
eps = 1e-06
lanes = 128
gather_bytes = 1 << 23


def unit_rows(values):
    values = values.astype(jnp.float32)
    norm = jnp.sqrt(jnp.sum(values * values, axis=1, keepdims=True) + eps)
    return (values / norm).astype(jnp.bfloat16)


def inner_rows(left, right):
    return lax.dot_general(
        left, right, (((1,), (1,)), ((), ())), preferred_element_type=jnp.float32
    )


def inner_cols(left, right):
    return lax.dot_general(
        left, right, (((0,), (0,)), ((), ())), preferred_element_type=jnp.float32
    )


def bits_down(count):
    return [1 << b for b in reversed(range(count.bit_length() - 1))]


def swap(values, axis, bit):
    count = lax.axis_size(axis)
    return lax.ppermute(values, axis, [(i, i ^ bit) for i in range(count)])


def spread(values, steps):
    pieces = [values]
    for axis, bit in steps:
        if len(pieces) > 1:
            values = jnp.concatenate(pieces, axis=0)
            pieces = [values]
        pieces.append(swap(values, axis, bit))
    return pieces


def own_half(values, start, half):
    return lax.dynamic_slice_in_dim(values, start, half, 0)


def in_vmem(count):
    return [pl.BlockSpec(memory_space=pltpu.VMEM)] * count


def loss_step(raw, teach_b, capt_all, place, total):
    rows, width = raw.shape

    def kernel(raw_ref, teach_ref, capt_ref, place_ref, out_ref):
        raw = raw_ref[...]
        norm = jnp.sqrt(jnp.sum(raw * raw, axis=1, keepdims=True) + eps)
        student = raw / norm
        stacked = jnp.concatenate([teach_ref[...], student.astype(jnp.bfloat16)], axis=0)
        scores = inner_rows(stacked, capt_ref[...])
        tlog = teacher_scale * scores[:rows]
        slog = student_scale * scores[rows:]
        texp = jnp.exp(tlog)
        sexp = jnp.exp(slog)
        hit = lax.broadcasted_iota(jnp.int32, tlog.shape, 1) == place_ref[...]
        zt_sum = jnp.sum(texp, axis=1, keepdims=True)
        zs_sum = jnp.sum(sexp, axis=1, keepdims=True)
        acc_sum = jnp.sum(texp * (tlog - slog), axis=1, keepdims=True)
        spair = jnp.sum(jnp.where(hit, slog, 0.0), axis=1, keepdims=True)
        coef = 2.0 / zs_sum * sexp - 1.0 / zt_sum * texp - jnp.where(hit, 1.0, 0.0)
        dstud = jnp.dot(
            coef.astype(jnp.bfloat16), capt_ref[...], preferred_element_type=jnp.float32
        ) * (student_scale / total)
        along = jnp.sum(student * dstud, axis=1, keepdims=True)
        draw = ((dstud - student * along) / norm).astype(jnp.bfloat16)
        for index in range(width // lanes):
            out_ref[index * rows : (index + 1) * rows, :] = draw[
                :, index * lanes : (index + 1) * lanes
            ]
        loss = acc_sum / zt_sum - jnp.log(zt_sum) + 2.0 * jnp.log(zs_sum) - spair
        rest = jnp.broadcast_to(jnp.sum(loss, axis=0, keepdims=True), (8, lanes))
        row = lax.broadcasted_iota(jnp.int32, rest.shape, 0)
        lane = lax.broadcasted_iota(jnp.int32, rest.shape, 1)
        packed = jnp.zeros_like(rest)
        for index in range(3):
            term = rest.astype(jnp.bfloat16).astype(jnp.float32)
            packed = jnp.where((row == 0) & (lane == index), term, packed)
            rest = rest - term
        out_ref[width // lanes * rows :, :] = packed.astype(jnp.bfloat16)

    return pl.pallas_call(
        kernel,
        out_shape=jax.ShapeDtypeStruct((rows * width // lanes + 8, lanes), jnp.bfloat16),
        in_specs=in_vmem(4),
        out_specs=in_vmem(1)[0],
        compiler_params=pltpu.CompilerParams(vmem_limit_bytes=16 << 20),
        name="loss_step",
    )(raw, teach_b, capt_all, place)


def unpacked(ref, rows, width):
    step = rows * width // lanes + 8
    draws, tiles = [], []
    for base in range(0, ref.shape[0], step):
        draws.append(
            jnp.concatenate(
                [ref[base + k * rows : base + (k + 1) * rows, :] for k in range(width // lanes)],
                axis=1,
            )
        )
        tiles.append(ref[base + step - 8 : base + step, :].astype(jnp.float32))
    return jnp.concatenate(draws, axis=0), sum(tiles)


def first_grads(packed, starts, last_starts, feats, hidden_t, slope_t, weight, rows):
    units, width, depth = hidden_t.shape[0], weight.shape[1], feats[0].shape[1]
    step = rows * width // lanes + 8
    bounds = [0]
    for values in feats:
        bounds.append(bounds[-1] + values.shape[0])
    stops = [start + values.shape[0] // step * rows for start, values in zip(starts, packed)]
    last_stops = [start + rest for start, rest in zip(last_starts, [bounds[-1] // 2 - stops[0]] * 2)]

    def kernel(*refs):
        packed_refs, feat_refs = refs[: len(packed)], refs[len(packed) : len(packed) + len(feats)]
        hidden_ref, slope_ref, weight_ref, first_ref, second_ref, tile_ref, last_ref = refs[-7:]

        def feat_rows(start, stop):
            return jnp.concatenate(
                [
                    ref[max(low, start) - low : min(high, stop) - low, :]
                    for ref, low, high in zip(feat_refs, bounds, bounds[1:])
                    if max(low, start) < min(high, stop)
                ],
                axis=0,
            )

        first, second, tile = [], [], []
        for ref, start, stop in zip(packed_refs, starts, stops):
            draw, part = unpacked(ref, rows, width)
            dpre = (inner_rows(weight_ref[...], draw) * slope_ref[:, start:stop]).astype(
                jnp.bfloat16
            )
            second.append(
                jnp.dot(hidden_ref[:, start:stop], draw, preferred_element_type=jnp.float32)
            )
            first.append(
                jnp.dot(dpre, feat_rows(start, stop), preferred_element_type=jnp.float32)
            )
            tile.append(part)
        first_ref[...] = sum(first).T
        second_ref[...] = sum(second)
        tile_ref[...] = sum(tile)
        last = [feat_rows(start, stop) for start, stop in zip(last_starts, last_stops)]
        last_ref[...] = jnp.concatenate(last, axis=0).T

    count = sum(stop - start for start, stop in zip(last_starts, last_stops))
    return pl.pallas_call(
        kernel,
        out_shape=(
            jax.ShapeDtypeStruct((depth, units), jnp.float32),
            jax.ShapeDtypeStruct((units, width), jnp.float32),
            jax.ShapeDtypeStruct((8, lanes), jnp.float32),
            jax.ShapeDtypeStruct((depth, count), jnp.bfloat16),
        ),
        in_specs=in_vmem(len(packed) + len(feats) + 3),
        out_specs=in_vmem(4),
        compiler_params=pltpu.CompilerParams(vmem_limit_bytes=16 << 20),
        name="first_grads",
    )(*packed, *feats, hidden_t, slope_t, weight)


def last_grads(packed, starts, sums, hidden_t, slope_t, weight, rows, total):
    units, width, depth = hidden_t.shape[0], weight.shape[1], sums[0].shape[0]

    def kernel(*refs):
        packed_refs = refs[: len(packed)]
        hidden_ref, slope_ref, weight_ref, first_ref, second_ref, tile_ref, feats_ref = refs[
            len(packed) : -3
        ]
        loss_out, first_out, second_out = refs[-3:]
        draws, tiles = zip(*(unpacked(ref, rows, width) for ref in packed_refs))
        draw = jnp.concatenate(draws, axis=0)
        columns = [
            slice(start, start + values.shape[0]) for start, values in zip(starts, draws)
        ]
        slope = jnp.concatenate([slope_ref[:, part] for part in columns], axis=1)
        hidden = jnp.concatenate([hidden_ref[:, part] for part in columns], axis=1)
        dpre = (inner_rows(weight_ref[...], draw) * slope).astype(jnp.bfloat16)
        first_out[...] = first_ref[...] + inner_rows(feats_ref[...], dpre)
        second_out[...] = second_ref[...] + jnp.dot(
            hidden, draw, preferred_element_type=jnp.float32
        )
        loss_out[0, 0] = jnp.sum(tile_ref[...] + sum(tiles)) / total

    return pl.pallas_call(
        kernel,
        out_shape=(
            jax.ShapeDtypeStruct((1, 1), jnp.float32),
            jax.ShapeDtypeStruct((depth, units), jnp.float32),
            jax.ShapeDtypeStruct((units, width), jnp.float32),
        ),
        in_specs=in_vmem(len(packed) + 7),
        out_specs=[pl.BlockSpec(memory_space=pltpu.SMEM)] + in_vmem(2),
        compiler_params=pltpu.CompilerParams(vmem_limit_bytes=16 << 20),
        name="last_grads",
    )(*packed, hidden_t, slope_t, weight, *sums)


def stage(values):
    def kernel(values_ref, copy_ref):
        copy_ref[...] = values_ref[...]

    return pl.pallas_call(
        kernel,
        out_shape=jax.ShapeDtypeStruct(values.shape, values.dtype),
        in_specs=[pl.BlockSpec(memory_space=pltpu.VMEM)],
        out_specs=pl.BlockSpec(memory_space=pltpu.VMEM),
        compiler_params=pltpu.CompilerParams(vmem_limit_bytes=1 << 20),
        name="stage",
    )(values)


def gelu_exact(values):
    return jax.nn.gelu(values, approximate=False)


def body(clip_feats, teacher_audio, teacher_text, w_first, w_second, pairing):
    rows = clip_feats.shape[0]
    wide_size = lax.axis_size("wide")
    mp_size = lax.axis_size("mp")
    total = rows * wide_size
    part = teacher_text.shape[0]
    half = rows // 2
    wide_bits = bits_down(wide_size)
    mp_bits = bits_down(mp_size)
    own_start = lax.axis_index("mp") % 2 * half

    far_bits, near_bit = wide_bits[:-1], wide_bits[-1]
    far_steps = [("wide", bit) for bit in far_bits]
    gathers = gathers_rows(total, clip_feats.shape[1])

    block = jnp.concatenate(spread(teacher_text, far_steps), axis=0)
    across = swap(block, "wide", near_bit)
    beside = swap(block, "mp", mp_bits[0])
    corner = swap(across, "mp", mp_bits[0])
    most = jnp.concatenate([unit_rows(block), unit_rows(beside), unit_rows(across)], axis=0)
    corner = unit_rows(corner)
    capt_all = jnp.concatenate([most, corner, swap(most, "mp", 1), swap(corner, "mp", 1)], axis=0)
    places = [("wide", bit) for bit in far_bits]
    places += [("mp", mp_bits[0]), ("wide", near_bit), ("mp", 1)]

    pre_act = jnp.dot(clip_feats, w_first, preferred_element_type=jnp.float32)
    hidden = gelu_exact(pre_act).astype(jnp.bfloat16)
    raw = jnp.dot(hidden, w_second, preferred_element_type=jnp.float32)
    own = own_half(raw, own_start, half)
    raw = own + swap(own_half(raw, half - own_start, half), "mp", 1)
    raw = raw + swap(raw, "mp", mp_bits[0])
    teach_b = unit_rows(own_half(teacher_audio, own_start, half))

    place = places_of(own_half(pairing, own_start, half), part, places)

    if not gathers:
        return summed_grads(
            clip_feats, own_start, hidden, pre_act, raw, teach_b, capt_all, place, w_second, total
        )

    draw = loss_step(raw, teach_b, capt_all, place, total)
    feats = spread(own_half(clip_feats, own_start, half), far_steps)
    feats = [
        jnp.concatenate(feats, axis=0),
        swap(jnp.concatenate(feats[:-1], axis=0), "wide", near_bit),
        swap(feats[-1], "wide", near_bit),
    ]
    feats.append(swap(jnp.concatenate(feats, axis=0), "mp", 1))
    draws = spread(draw, far_steps)
    across = swap(jnp.concatenate(draws[:-1], axis=0), "wide", near_bit)
    last = swap(draws[-1], "wide", near_bit)
    most = jnp.concatenate([*draws, across], axis=0)
    most = [most, swap(most, "mp", 1)]
    last = [last, swap(last, "mp", 1)]
    pre_t = jnp.concatenate(
        [
            lax.dot_general(
                w_first, rows, (((0,), (1,)), ((), ())), preferred_element_type=jnp.float32
            )
            for rows in feats
        ],
        axis=1,
    )
    gelu_t, gelu_back = jax.vjp(gelu_exact, pre_t)
    slope_t = gelu_back(jnp.ones_like(pre_t))[0]
    hidden_t = gelu_t.astype(jnp.bfloat16)
    factors = (hidden_t, slope_t, stage(w_second))
    rest = rows_of(last[0], draw, half)
    starts = [0, total // 2]
    last_starts = [total // 2 - rest, total - rest]
    sums = first_grads(most, starts, last_starts, feats, *factors, half)
    loss, grad_first, grad_second = last_grads(last, last_starts, sums, *factors, half, total)
    return (loss[0, 0], grad_first, grad_second)


def rows_of(packed, block, half):
    return packed.shape[0] // block.shape[0] * half


def places_of(pair, part, places):
    mp_size = lax.axis_size("mp")
    differs = {
        "wide": (pair // (part * mp_size)) ^ lax.axis_index("wide"),
        "mp": (pair // part % mp_size) ^ lax.axis_index("mp"),
    }
    place = pair % part
    for index, (axis, bit) in enumerate(places):
        place = place + (part << index) * (differs[axis] // bit % 2)
    return place[:, None]


def summed_grads(
    clip_feats, own_start, hidden, pre_act, raw, teach_b, capt_all, place, w_second, total
):
    half = raw.shape[0]
    gelu_back = jax.vjp(gelu_exact, pre_act)[1]
    norm = jnp.sqrt(jnp.sum(raw * raw, axis=1, keepdims=True) + eps)
    student = raw / norm
    stud_b = student.astype(jnp.bfloat16)
    scores = inner_rows(jnp.concatenate([teach_b, stud_b], axis=0), capt_all)
    tlog = teacher_scale * scores[:half]
    slog = student_scale * scores[half:]
    hit = jnp.arange(total, dtype=jnp.int32)[None, :] == place
    texp = jnp.exp(tlog)
    sexp = jnp.exp(slog)
    zt_sum = jnp.sum(texp, axis=1)
    zs_sum = jnp.sum(sexp, axis=1)
    acc_sum = jnp.sum(texp * (tlog - slog), axis=1)
    spair = jnp.sum(jnp.where(hit, slog, 0.0), axis=1)
    loss = jnp.sum(acc_sum / zt_sum - jnp.log(zt_sum) + 2.0 * jnp.log(zs_sum) - spair)
    coef = (
        2.0 * sexp / zs_sum[:, None] - texp / zt_sum[:, None] - hit.astype(jnp.float32)
    ).astype(jnp.bfloat16)
    dstud = jnp.dot(coef, capt_all, preferred_element_type=jnp.float32) * (student_scale / total)
    draw = ((dstud - student * jnp.sum(student * dstud, axis=1, keepdims=True)) / norm).astype(
        jnp.bfloat16
    )

    draw = jnp.concatenate([draw, swap(draw, "mp", 1)], axis=0)
    draw = jnp.where(own_start > 0, jnp.roll(draw, half, axis=0), draw)
    grad_second = inner_cols(hidden, draw)
    dpre = gelu_back(inner_rows(draw, w_second))[0].astype(jnp.bfloat16)
    grad_first = inner_cols(clip_feats, dpre)
    tile = jnp.full((8, 128), loss, jnp.float32)
    loss = (tile + swap(tile, "mp", 1))[0, 0]
    grad_first, grad_second, loss = lax.psum((grad_first, grad_second, loss), "wide")
    return (loss / total, grad_first, grad_second)


def gathers_rows(total, depth):
    return 2 * total * depth <= gather_bytes


def solution(mesh):
    return jax.shard_map(
        body,
        mesh=mesh,
        in_specs=(
            P("wide", None),
            P("wide", None),
            P(("wide", "mp"), None),
            P(None, "mp"),
            P("mp", None),
            P("wide"),
        ),
        out_specs=(P(), P(None, "mp"), P("mp", None)),
        check_vma=False,
    )
```

profile of v0, /device:TPU:0, one launch (start us, length us, event | category | flops | bytes accessed | tf_op | source)
XLA Modules:
  0.0 54.0 jit_solution(13118343255656990727)
XLA Ops:
  0.6 4.1 %collective-permute-start.2 = (bf16[32,512]{1,0:T(8,128)(2,1)}, bf16[32,512]{1,0:T(8,128)(2,1)S(1)}, u32[]{:S(2)}, u32[]{:S(2)}) collective-permute-start(bf16[32,512]{1,0:T(8,128)(2,1)} %param.8), channel_id=1, source_target_pairs={{0,16},{4,20},{8,24},{12,28},{16,0},{20,4},{24,8},{28,12},{1,17},{... | collective-permute-start | bytes 98312 | tf_op jit(solution)/shard_map/ppermute | solution.py:39
  4.8 1.4 %fusion.26 = f32[128,512]{1,0:T(8,128)S(1)} fusion(bf16[128,512]{1,0:T(8,128)(2,1)} %values_ref.1, bf16[128,768]{1,0:T(8,128)(2,1)} %param.6, bf16[768,128]{1,0:T(8,128)(2,1)S(1)} %copy-done), kind=kOutput, calls=%fused_computation.68 | convolution fusion | flops 43008000 | bytes 786432 | tf_op jit(solution)/shard_map/dot_general | solution.py:263
  6.3 0.8 %copy-done.4 = bf16[128,768]{1,0:T(8,128)(2,1)S(1)} copy-done((bf16[128,768]{1,0:T(8,128)(2,1)S(1)}, bf16[128,768]{1,0:T(8,128)(2,1)}, u32[]{:S(2)}) %copy-start.4) | copy-done | bytes 196632
  7.2 0.9 %collective-permute-start.13 = (bf16[64,768]{1,0:T(8,128)(2,1)S(1)}, bf16[64,768]{1,0:T(8,128)(2,1)S(1)}, u32[]{:S(2)}, u32[]{:S(2)}) collective-permute-start(bf16[64,768]{1,0:T(8,128)(2,1)S(1)} %get-tuple-element.20), channel_id=1, source_target_pairs={{0,16},{4,20},{8,24},{12,28},{16,0},{20,4},{24,8},{28,12},{1,17},{... | collective-permute-start | bytes 294920 | tf_op jit(solution)/shard_map/ppermute | solution.py:39
  8.4 0.6 %copy-done.5 = s32[128]{0:T(128)S(1)} copy-done((s32[128]{0:T(128)S(1)}, s32[128]{0:T(128)}, u32[]{:S(2)}) %copy-start.5) | copy-done | bytes 536
  9.3 1.6 %collective-permute-start.3 = (bf16[64,512]{1,0:T(8,128)(2,1)S(1)}, bf16[64,512]{1,0:T(8,128)(2,1)S(1)}, u32[]{:S(2)}, u32[]{:S(2)}) collective-permute-start(bf16[64,512]{1,0:T(8,128)(2,1)S(1)} %pad_maximum_fusion.6), channel_id=1, source_target_pairs={{0,8},{4,12},{8,0},{12,4},{16,24},{20,28},{24,16},{28,20},{1,9},{5... | collective-permute-start | bytes 196616 | tf_op jit(solution)/shard_map/ppermute | solution.py:39
  10.9 3.4 %collective-permute-done.3 = bf16[64,512]{1,0:T(8,128)(2,1)S(1)} collective-permute-done((bf16[64,512]{1,0:T(8,128)(2,1)S(1)}, bf16[64,512]{1,0:T(8,128)(2,1)S(1)}, u32[]{:S(2)}, u32[]{:S(2)}) %collective-permute-start.3) | collective-permute-done | bytes 65568 | tf_op jit(solution)/shard_map/ppermute | solution.py:39
  14.4 1.6 %collective-permute-start.4 = (bf16[128,512]{1,0:T(8,128)(2,1)S(1)}, bf16[128,512]{1,0:T(8,128)(2,1)S(1)}, u32[]{:S(2)}, u32[]{:S(2)}) collective-permute-start(bf16[128,512]{1,0:T(8,128)(2,1)S(1)} %constant_dynamic-update-slice_fusion), channel_id=1, source_target_pairs={{0,2},{1,3},{2,0},{3,1},{4,6},{5,7},{6,4},{7,5},{8,10},{9,11},{10,... | collective-permute-start | bytes 393224 | tf_op jit(solution)/shard_map/ppermute | solution.py:39
  15.9 1.5 %collective-permute-start.5 = (bf16[128,512]{1,0:T(8,128)(2,1)S(1)}, bf16[128,512]{1,0:T(8,128)(2,1)S(1)}, u32[]{:S(2)}, u32[]{:S(2)}) collective-permute-start(bf16[128,512]{1,0:T(8,128)(2,1)S(1)} %constant_dynamic-update-slice_fusion), channel_id=1, source_target_pairs={{0,4},{4,0},{8,12},{12,8},{16,20},{20,16},{24,28},{28,24},{1,5},{5... | collective-permute-start | bytes 393224 | tf_op jit(solution)/shard_map/ppermute | solution.py:39
  17.6 1.0 %collective-permute-start.14 = (bf16[128,768]{1,0:T(8,128)(2,1)S(1)}, bf16[128,768]{1,0:T(8,128)(2,1)S(1)}, u32[]{:S(2)}, u32[]{:S(2)}) collective-permute-start(bf16[128,768]{1,0:T(8,128)(2,1)S(1)} %pad_maximum_fusion.4), channel_id=1, source_target_pairs={{0,8},{4,12},{8,0},{12,4},{16,24},{20,28},{24,16},{28,20},{1,9},{5... | collective-permute-start | bytes 589832 | tf_op jit(solution)/shard_map/ppermute | solution.py:39
  18.6 0.5 collective-permute-start.15
  19.1 0.6 %collective-permute-start.1 = (f32[64,512]{1,0:T(8,128)S(1)}, f32[64,512]{1,0:T(8,128)S(1)}, u32[]{:S(2)}, u32[]{:S(2)}) collective-permute-start(f32[64,512]{1,0:T(8,128)S(1)} %dynamic-slice_add_fusion), channel_id=1, source_target_pairs={{0,2},{1,3},{2,0},{3,1},{4,6},{5,7},{6,4},{7,5},{8,10},{9,11},{10,... | collective-permute-start | bytes 393224 | tf_op jit(solution)/shard_map/ppermute | solution.py:39
  19.9 2.5 %collective-permute-done.5 = bf16[128,512]{1,0:T(8,128)(2,1)S(1)} collective-permute-done((bf16[128,512]{1,0:T(8,128)(2,1)S(1)}, bf16[128,512]{1,0:T(8,128)(2,1)S(1)}, u32[]{:S(2)}, u32[]{:S(2)}) %collective-permute-start.5) | collective-permute-done | bytes 131104 | tf_op jit(solution)/shard_map/ppermute | solution.py:39
  22.8 0.6 %collective-permute-start.6 = (bf16[128,512]{1,0:T(8,128)(2,1)S(1)}, bf16[128,512]{1,0:T(8,128)(2,1)S(1)}, u32[]{:S(2)}, u32[]{:S(2)}) collective-permute-start(bf16[128,512]{1,0:T(8,128)(2,1)S(1)} %collective-permute-done.5), channel_id=1, source_target_pairs={{0,2},{1,3},{2,0},{3,1},{4,6},{5,7},{6,4},{7,5},{8,10},{9,11},{10,... | collective-permute-start | bytes 393224 | tf_op jit(solution)/shard_map/ppermute | solution.py:39
  23.4 0.8 %collective-permute-done.1 = f32[64,512]{1,0:T(8,128)S(1)} collective-permute-done((f32[64,512]{1,0:T(8,128)S(1)}, f32[64,512]{1,0:T(8,128)S(1)}, u32[]{:S(2)}, u32[]{:S(2)}) %collective-permute-start.1) | collective-permute-done | bytes 131104 | tf_op jit(solution)/shard_map/ppermute | solution.py:39
  24.2 1.6 %collective-permute-start.16 = (bf16[128,768]{1,0:T(8,128)(2,1)S(1)}, bf16[128,768]{1,0:T(8,128)(2,1)S(1)}, u32[]{:S(2)}, u32[]{:S(2)}) collective-permute-start(bf16[128,768]{1,0:T(8,128)(2,1)S(1)} %collective-permute-done.14), channel_id=1, source_target_pairs={{0,4},{4,0},{8,12},{12,8},{16,20},{20,16},{24,28},{28,24},{1,5},{5... | collective-permute-start | bytes 589832 | tf_op jit(solution)/shard_map/ppermute | solution.py:39
  25.8 0.3 convolution_bitcast_fusion.1
  26.1 0.3 convolution_bitcast_fusion.3
  26.4 2.2 %collective-permute-done.6 = bf16[128,512]{1,0:T(8,128)(2,1)S(1)} collective-permute-done((bf16[128,512]{1,0:T(8,128)(2,1)S(1)}, bf16[128,512]{1,0:T(8,128)(2,1)S(1)}, u32[]{:S(2)}, u32[]{:S(2)}) %collective-permute-start.6) | collective-permute-done | bytes 131104 | tf_op jit(solution)/shard_map/ppermute | solution.py:39
  29.0 1.4 %collective-permute-done.16.refs_4_ = bf16[128,768]{1,0:T(8,128)(2,1)S(1)} collective-permute-done((bf16[128,768]{1,0:T(8,128)(2,1)S(1)}, bf16[128,768]{1,0:T(8,128)(2,1)S(1)}, u32[]{:S(2)}, u32[]{:S(2)}) %collective-permute-start.16) | collective-permute-done | bytes 196640 | tf_op jit(solution)/shard_map/ppermute | solution.py:39
  30.6 1.0 %loss_step.1 = bf16[264,128]{1,0:T(8,128)(2,1)S(1)} custom-call(f32[64,512]{1,0:T(8,128)S(1)} %add.119.raw_ref, bf16[64,512]{1,0:T(8,128)(2,1)S(1)} %fusion.15.teach_ref, bf16[1024,512]{1,0:T(8,128)(2,1)S(1)} %constant_dynamic-update-slice_fusion.3.capt_ref, s32[64,1]{1,0:T(8,128)S(1)} %copy.9.place_ref), custom_call_target="tpu_custom_call" | custom-call | tf_op jit(solution)/shard_map/loss_step/pallas_call | solution.py:99
  31.6 3.5 %collective-permute-start.9 = (bf16[264,128]{1,0:T(8,128)(2,1)S(1)}, bf16[264,128]{1,0:T(8,128)(2,1)S(1)}, u32[]{:S(2)}, u32[]{:S(2)}) collective-permute-start(bf16[264,128]{1,0:T(8,128)(2,1)S(1)} %loss_step.1), channel_id=1, source_target_pairs={{0,16},{4,20},{8,24},{12,28},{16,0},{20,4},{24,8},{28,12},{1,17},{... | collective-permute-start | bytes 202760 | tf_op jit(solution)/shard_map/ppermute | solution.py:39
  35.2 4.2 %collective-permute-done.9 = bf16[264,128]{1,0:T(8,128)(2,1)S(1)} collective-permute-done((bf16[264,128]{1,0:T(8,128)(2,1)S(1)}, bf16[264,128]{1,0:T(8,128)(2,1)S(1)}, u32[]{:S(2)}, u32[]{:S(2)}) %collective-permute-start.9) | collective-permute-done | bytes 67616 | tf_op jit(solution)/shard_map/ppermute | solution.py:39
  39.4 1.6 %collective-permute-start.18 = (bf16[528,128]{1,0:T(8,128)(2,1)S(1)}, bf16[528,128]{1,0:T(8,128)(2,1)S(1)}, u32[]{:S(2)}, u32[]{:S(2)}) collective-permute-start(bf16[528,128]{1,0:T(8,128)(2,1)S(1)} %pad_maximum_fusion.5), channel_id=1, source_target_pairs={{0,4},{4,0},{8,12},{12,8},{16,20},{20,16},{24,28},{28,24},{1,5},{5... | collective-permute-start | bytes 405512 | tf_op jit(solution)/shard_map/ppermute | solution.py:39
  41.0 0.3 convolution_bitcast_fusion.2
  41.3 3.7 %collective-permute-done.10 = bf16[528,128]{1,0:T(8,128)(2,1)S(1)} collective-permute-done((bf16[528,128]{1,0:T(8,128)(2,1)S(1)}, bf16[528,128]{1,0:T(8,128)(2,1)S(1)}, u32[]{:S(2)}, u32[]{:S(2)}) %collective-permute-start.10) | collective-permute-done | bytes 135200 | tf_op jit(solution)/shard_map/ppermute | solution.py:39
  45.0 1.4 %collective-permute-start.11 = (bf16[528,128]{1,0:T(8,128)(2,1)S(1)}, bf16[528,128]{1,0:T(8,128)(2,1)S(1)}, u32[]{:S(2)}, u32[]{:S(2)}) collective-permute-start(bf16[528,128]{1,0:T(8,128)(2,1)S(1)} %collective-permute-done.10), channel_id=1, source_target_pairs={{0,4},{4,0},{8,12},{12,8},{16,20},{20,16},{24,28},{28,24},{1,5},{5... | collective-permute-start | bytes 405512 | tf_op jit(solution)/shard_map/ppermute | solution.py:39
  46.5 3.5 %collective-permute-done.11.refs_0_ = bf16[528,128]{1,0:T(8,128)(2,1)S(1)} collective-permute-done((bf16[528,128]{1,0:T(8,128)(2,1)S(1)}, bf16[528,128]{1,0:T(8,128)(2,1)S(1)}, u32[]{:S(2)}, u32[]{:S(2)}) %collective-permute-start.11) | collective-permute-done | bytes 135200 | tf_op jit(solution)/shard_map/ppermute | solution.py:39
  50.0 0.4 convolution_bitcast_fusion
  50.4 1.2 %multiply_add_fusion = (f32[128,1024]{1,0:T(8,128)S(1)}, f32[128,1024]{1,0:T(8,128)S(1)}) fusion(f32[128,512]{1,0:T(8,128)S(1)} %convolution_bitcast_fusion, f32[128,128]{1,0:T(8,128)S(1)} %convolution_bitcast_fusion.2, f32[128,128]{1,0:T(8,128)S(1)} %convolution_bitcast_fusion.3, f32[128,256]{1,0:T(8,128)S(1)} %convolution_bitcast_fusion.1), kind=kLoop, calls=%fused_computation.7 | loop fusion | flops 9306112 | bytes 1572864 | tf_op jit(solution)/shard_map/transpose(jvp())/add_any | solution.py:233
  51.7 0.9 %first_grads.1 = (f32[768,128]{1,0:T(8,128)S(1)}, f32[128,512]{1,0:T(8,128)S(1)}, f32[8,128]{1,0:T(8,128)S(1)}, bf16[768,256]{1,0:T(8,128)(2,1)S(1)}) custom-call(bf16[1584,128]{1,0:T(8,128)(2,1)S(1)} %pad_maximum_fusion.1.refs_0_, bf16[1584,128]{1,0:T(8,128)(2,1)S(1)} %collective-permute-done.19.refs_1_, bf16[256,768]{1,0:T(8,128)(2,1)S(1)} %pad_maximum_fusion.3.refs_2_, ...), custom_call_target="tpu_custom_call" | custom-call | tf_op jit(solution)/shard_map/first_grads/pallas_call | solution.py:166
  52.6 1.4 %last_grads.1 = (f32[1,1]{1,0:T(1,128)}, f32[768,128]{1,0:T(8,128)}, f32[128,512]{1,0:T(8,128)}) custom-call(bf16[528,128]{1,0:T(8,128)(2,1)S(1)} %collective-permute-done.11.refs_0_, bf16[528,128]{1,0:T(8,128)(2,1)S(1)} %collective-permute-done.12.refs_1_, bf16[128,1024]{1,0:T(8,128)(2,1)S(1)} %multiply_convert_fusion.refs_6_.refs_2_, ...), custom_call_target="tpu_custom_call" | custom-call | tf_op jit(solution)/shard_map/last_grads/pallas_call | solution.py:204
  (67 shorter events, 2.2 us)
Async XLA Ops:
  0.6 4.1 %copy-start = (bf16[768,128]{1,0:T(8,128)(2,1)S(1)}, bf16[768,128]{1,0:T(8,128)(2,1)}, u32[]{:S(2)}) copy-start(bf16[768,128]{1,0:T(8,128)(2,1)} %param.9) | copy-start | bytes 589828
  0.6 8.6 %collective-permute-start.2 = (bf16[32,512]{1,0:T(8,128)(2,1)}, bf16[32,512]{1,0:T(8,128)(2,1)S(1)}, u32[]{:S(2)}, u32[]{:S(2)}) collective-permute-start(bf16[32,512]{1,0:T(8,128)(2,1)} %param.8), channel_id=1, source_target_pairs={{0,16},{4,20},{8,24},{12,28},{16,0},{20,4},{24,8},{28,12},{1,17},{... | collective-permute-start | bytes 98312 | tf_op jit(solution)/shard_map/ppermute | solution.py:39
  6.2 0.9 %copy-start.4 = (bf16[128,768]{1,0:T(8,128)(2,1)S(1)}, bf16[128,768]{1,0:T(8,128)(2,1)}, u32[]{:S(2)}) copy-start(bf16[128,768]{1,0:T(8,128)(2,1)} %param.6) | copy-start | bytes 589828
  6.2 12.9 %collective-permute-start = (f32[64,512]{1,0:T(8,128)S(1)}, f32[64,512]{1,0:T(8,128)S(1)}, u32[]{:S(2)}, u32[]{:S(2)}) collective-permute-start(f32[64,512]{1,0:T(8,128)S(1)} %constant_dynamic-slice_fusion.1), channel_id=1, source_target_pairs={{0,1},{1,0},{2,3},{3,2},{4,5},{5,4},{6,7},{7,6},{8,9},{9,8},{10,11... | collective-permute-start | bytes 393224 | tf_op jit(solution)/shard_map/ppermute | solution.py:39
  7.2 1.0 %copy-start.3 = (bf16[32,512]{1,0:T(8,128)(2,1)S(1)}, bf16[32,512]{1,0:T(8,128)(2,1)}, u32[]{:S(2)}) copy-start(bf16[32,512]{1,0:T(8,128)(2,1)} %param.8) | copy-start | bytes 98308
  7.2 1.0 %copy-start.2 = (bf16[128,512]{1,0:T(8,128)(2,1)S(1)}, bf16[128,512]{1,0:T(8,128)(2,1)}, u32[]{:S(2)}) copy-start(bf16[128,512]{1,0:T(8,128)(2,1)} %param.7) | copy-start | bytes 393220
  7.2 1.9 %copy-start.1 = (bf16[128,512]{1,0:T(8,128)(2,1)S(1)}, bf16[128,512]{1,0:T(8,128)(2,1)}, u32[]{:S(2)}) copy-start(bf16[128,512]{1,0:T(8,128)(2,1)} %values_ref.1) | copy-start | bytes 393220
  7.2 10.4 %collective-permute-start.13 = (bf16[64,768]{1,0:T(8,128)(2,1)S(1)}, bf16[64,768]{1,0:T(8,128)(2,1)S(1)}, u32[]{:S(2)}, u32[]{:S(2)}) collective-permute-start(bf16[64,768]{1,0:T(8,128)(2,1)S(1)} %get-tuple-element.20), channel_id=1, source_target_pairs={{0,16},{4,20},{8,24},{12,28},{16,0},{20,4},{24,8},{28,12},{1,17},{... | collective-permute-start | bytes 294920 | tf_op jit(solution)/shard_map/ppermute | solution.py:39
  8.4 0.7 %copy-start.5 = (s32[128]{0:T(128)S(1)}, s32[128]{0:T(128)}, u32[]{:S(2)}) copy-start(s32[128]{0:T(128)} %param.11) | copy-start | bytes 1540
  9.3 5.0 %collective-permute-start.3 = (bf16[64,512]{1,0:T(8,128)(2,1)S(1)}, bf16[64,512]{1,0:T(8,128)(2,1)S(1)}, u32[]{:S(2)}, u32[]{:S(2)}) collective-permute-start(bf16[64,512]{1,0:T(8,128)(2,1)S(1)} %pad_maximum_fusion.6), channel_id=1, source_target_pairs={{0,8},{4,12},{8,0},{12,4},{16,24},{20,28},{24,16},{28,20},{1,9},{5... | collective-permute-start | bytes 196616 | tf_op jit(solution)/shard_map/ppermute | solution.py:39
  14.4 5.3 %collective-permute-start.4 = (bf16[128,512]{1,0:T(8,128)(2,1)S(1)}, bf16[128,512]{1,0:T(8,128)(2,1)S(1)}, u32[]{:S(2)}, u32[]{:S(2)}) collective-permute-start(bf16[128,512]{1,0:T(8,128)(2,1)S(1)} %constant_dynamic-update-slice_fusion), channel_id=1, source_target_pairs={{0,2},{1,3},{2,0},{3,1},{4,6},{5,7},{6,4},{7,5},{8,10},{9,11},{10,... | collective-permute-start | bytes 393224 | tf_op jit(solution)/shard_map/ppermute | solution.py:39
  15.9 6.4 %collective-permute-start.5 = (bf16[128,512]{1,0:T(8,128)(2,1)S(1)}, bf16[128,512]{1,0:T(8,128)(2,1)S(1)}, u32[]{:S(2)}, u32[]{:S(2)}) collective-permute-start(bf16[128,512]{1,0:T(8,128)(2,1)S(1)} %constant_dynamic-update-slice_fusion), channel_id=1, source_target_pairs={{0,4},{4,0},{8,12},{12,8},{16,20},{20,16},{24,28},{28,24},{1,5},{5... | collective-permute-start | bytes 393224 | tf_op jit(solution)/shard_map/ppermute | solution.py:39
  17.6 6.6 %collective-permute-start.14 = (bf16[128,768]{1,0:T(8,128)(2,1)S(1)}, bf16[128,768]{1,0:T(8,128)(2,1)S(1)}, u32[]{:S(2)}, u32[]{:S(2)}) collective-permute-start(bf16[128,768]{1,0:T(8,128)(2,1)S(1)} %pad_maximum_fusion.4), channel_id=1, source_target_pairs={{0,8},{4,12},{8,0},{12,4},{16,24},{20,28},{24,16},{28,20},{1,9},{5... | collective-permute-start | bytes 589832 | tf_op jit(solution)/shard_map/ppermute | solution.py:39
  18.6 7.5 %collective-permute-start.15 = (bf16[128,768]{1,0:T(8,128)(2,1)S(1)}, bf16[128,768]{1,0:T(8,128)(2,1)S(1)}, u32[]{:S(2)}, u32[]{:S(2)}) collective-permute-start(bf16[128,768]{1,0:T(8,128)(2,1)S(1)} %pad_maximum_fusion.4), channel_id=1, source_target_pairs={{0,4},{4,0},{8,12},{12,8},{16,20},{20,16},{24,28},{28,24},{1,5},{5... | collective-permute-start | bytes 589832 | tf_op jit(solution)/shard_map/ppermute | solution.py:39
  19.1 5.0 %collective-permute-start.1 = (f32[64,512]{1,0:T(8,128)S(1)}, f32[64,512]{1,0:T(8,128)S(1)}, u32[]{:S(2)}, u32[]{:S(2)}) collective-permute-start(f32[64,512]{1,0:T(8,128)S(1)} %dynamic-slice_add_fusion), channel_id=1, source_target_pairs={{0,2},{1,3},{2,0},{3,1},{4,6},{5,7},{6,4},{7,5},{8,10},{9,11},{10,... | collective-permute-start | bytes 393224 | tf_op jit(solution)/shard_map/ppermute | solution.py:39
  22.7 7.8 %collective-permute-start.7 = (bf16[384,512]{1,0:T(8,128)(2,1)S(1)}, bf16[384,512]{1,0:T(8,128)(2,1)S(1)}, u32[]{:S(2)}, u32[]{:S(2)}) collective-permute-start(bf16[384,512]{1,0:T(8,128)(2,1)S(1)} %pad_maximum_fusion.2), channel_id=1, source_target_pairs={{0,1},{1,0},{2,3},{3,2},{4,5},{5,4},{6,7},{7,6},{8,9},{9,8},{10,11... | collective-permute-start | bytes 1179656 | tf_op jit(solution)/shard_map/ppermute | solution.py:39
  22.8 5.9 %collective-permute-start.6 = (bf16[128,512]{1,0:T(8,128)(2,1)S(1)}, bf16[128,512]{1,0:T(8,128)(2,1)S(1)}, u32[]{:S(2)}, u32[]{:S(2)}) collective-permute-start(bf16[128,512]{1,0:T(8,128)(2,1)S(1)} %collective-permute-done.5), channel_id=1, source_target_pairs={{0,2},{1,3},{2,0},{3,1},{4,6},{5,7},{6,4},{7,5},{8,10},{9,11},{10,... | collective-permute-start | bytes 393224 | tf_op jit(solution)/shard_map/ppermute | solution.py:39
  24.2 6.2 %collective-permute-start.16 = (bf16[128,768]{1,0:T(8,128)(2,1)S(1)}, bf16[128,768]{1,0:T(8,128)(2,1)S(1)}, u32[]{:S(2)}, u32[]{:S(2)}) collective-permute-start(bf16[128,768]{1,0:T(8,128)(2,1)S(1)} %collective-permute-done.14), channel_id=1, source_target_pairs={{0,4},{4,0},{8,12},{12,8},{16,20},{20,16},{24,28},{28,24},{1,5},{5... | collective-permute-start | bytes 589832 | tf_op jit(solution)/shard_map/ppermute | solution.py:39
  28.9 1.7 %collective-permute-start.8 = (bf16[128,512]{1,0:T(8,128)(2,1)S(1)}, bf16[128,512]{1,0:T(8,128)(2,1)S(1)}, u32[]{:S(2)}, u32[]{:S(2)}) collective-permute-start(bf16[128,512]{1,0:T(8,128)(2,1)S(1)} %get-tuple-element.22), channel_id=1, source_target_pairs={{0,1},{1,0},{2,3},{3,2},{4,5},{5,4},{6,7},{7,6},{8,9},{9,8},{10,11... | collective-permute-start | bytes 393224 | tf_op jit(solution)/shard_map/ppermute | solution.py:39
  30.4 19.6 %collective-permute-start.17 = (bf16[512,768]{1,0:T(8,128)(2,1)S(1)}, bf16[512,768]{1,0:T(8,128)(2,1)S(1)}, u32[]{:S(2)}, u32[]{:S(2)}) collective-permute-start(bf16[512,768]{1,0:T(8,128)(2,1)S(1)} %constant_dynamic-update-slice_fusion.9), channel_id=1, source_target_pairs={{0,1},{1,0},{2,3},{3,2},{4,5},{5,4},{6,7},{7,6},{8,9},{9,8},{10,11... | collective-permute-start | bytes 2359304 | tf_op jit(solution)/shard_map/ppermute | solution.py:39
  31.6 7.7 %collective-permute-start.9 = (bf16[264,128]{1,0:T(8,128)(2,1)S(1)}, bf16[264,128]{1,0:T(8,128)(2,1)S(1)}, u32[]{:S(2)}, u32[]{:S(2)}) collective-permute-start(bf16[264,128]{1,0:T(8,128)(2,1)S(1)} %loss_step.1), channel_id=1, source_target_pairs={{0,16},{4,20},{8,24},{12,28},{16,0},{20,4},{24,8},{28,12},{1,17},{... | collective-permute-start | bytes 202760 | tf_op jit(solution)/shard_map/ppermute | solution.py:39
  39.4 5.7 %collective-permute-start.10 = (bf16[528,128]{1,0:T(8,128)(2,1)S(1)}, bf16[528,128]{1,0:T(8,128)(2,1)S(1)}, u32[]{:S(2)}, u32[]{:S(2)}) collective-permute-start(bf16[528,128]{1,0:T(8,128)(2,1)S(1)} %pad_maximum_fusion.5), channel_id=1, source_target_pairs={{0,8},{4,12},{8,0},{12,4},{16,24},{20,28},{24,16},{28,20},{1,9},{5... | collective-permute-start | bytes 405512 | tf_op jit(solution)/shard_map/ppermute | solution.py:39
  39.4 7.0 %collective-permute-start.18 = (bf16[528,128]{1,0:T(8,128)(2,1)S(1)}, bf16[528,128]{1,0:T(8,128)(2,1)S(1)}, u32[]{:S(2)}, u32[]{:S(2)}) collective-permute-start(bf16[528,128]{1,0:T(8,128)(2,1)S(1)} %pad_maximum_fusion.5), channel_id=1, source_target_pairs={{0,4},{4,0},{8,12},{12,8},{16,20},{20,16},{24,28},{28,24},{1,5},{5... | collective-permute-start | bytes 405512 | tf_op jit(solution)/shard_map/ppermute | solution.py:39
  45.0 5.0 %collective-permute-start.11 = (bf16[528,128]{1,0:T(8,128)(2,1)S(1)}, bf16[528,128]{1,0:T(8,128)(2,1)S(1)}, u32[]{:S(2)}, u32[]{:S(2)}) collective-permute-start(bf16[528,128]{1,0:T(8,128)(2,1)S(1)} %collective-permute-done.10), channel_id=1, source_target_pairs={{0,4},{4,0},{8,12},{12,8},{16,20},{20,16},{24,28},{28,24},{1,5},{5... | collective-permute-start | bytes 405512 | tf_op jit(solution)/shard_map/ppermute | solution.py:39
  46.4 5.3 %collective-permute-start.19 = (bf16[1584,128]{1,0:T(8,128)(2,1)S(1)}, bf16[1584,128]{1,0:T(8,128)(2,1)S(1)}, u32[]{:S(2)}, u32[]{:S(2)}) collective-permute-start(bf16[1584,128]{1,0:T(8,128)(2,1)S(1)} %pad_maximum_fusion.1.refs_0_), channel_id=1, source_target_pairs={{0,1},{1,0},{2,3},{3,2},{4,5},{5,4},{6,7},{7,6},{8,9},{9,8},{10,11... | collective-permute-start | bytes 1216520 | tf_op jit(solution)/shard_map/ppermute | solution.py:39
  50.0 2.6 %collective-permute-start.12 = (bf16[528,128]{1,0:T(8,128)(2,1)S(1)}, bf16[528,128]{1,0:T(8,128)(2,1)S(1)}, u32[]{:S(2)}, u32[]{:S(2)}) collective-permute-start(bf16[528,128]{1,0:T(8,128)(2,1)S(1)} %collective-permute-done.11.refs_0_), channel_id=1, source_target_pairs={{0,1},{1,0},{2,3},{3,2},{4,5},{5,4},{6,7},{7,6},{8,9},{9,8},{10,11... | collective-permute-start | bytes 405512 | tf_op jit(solution)/shard_map/ppermute | solution.py:39
where the time goes:
time: 54.2 us; the launch traced here: 54 us
  waiting for transfers between devices  21.7 us (40%)
  starting transfers between devices  21 us (39%)
  Pallas kernels  3.33 us (6%)
  matrix products  2.67 us (5%)
  other arithmetic  2.6 us (5%)
  local copies, waits for them, and re-layouts  1.72 us (3%)
  between operations  1.01 us (2%)
    ppermute x20, waiting for transfers between devices, swap(): return lax.ppermute(values, axis, [(i, i ^ bit) for i in range(count)])  21.7 us
    ppermute x20, starting transfers between devices, swap(): return lax.ppermute(values, axis, [(i, i ^ bit) for i in range(count)])  21 us
    unnamed x19, local copies, waits for them, and re-layouts  1.59 us
    dot_general x1, matrix products, body(): raw = jnp.dot(hidden, w_second, preferred_element_type=jnp.float32)  1.44 us
    pallas_call x1, Pallas kernels, last_grads(): pl.pallas_call(kernel, out_shape=(jax.ShapeDtypeStruct((1, 1), jnp.float3...  1.39 us
    dot_general x4, matrix products, body(): lax.dot_general(w_first, rows, (((0,), (1,)), ((), ())), preferred_elemen...  1.23 us
    add_any x1, other arithmetic, gelu_exact(): return jax.nn.gelu(values, approximate=False)  1.17 us
  transfers between devices with their start and end apart: 20, of which 8 were waited for; matrix products, arithmetic and copies ran while one was open for 10% of the time, Pallas kernels for 4%

commit v1 on v0

--- a/solution.py
+++ b/solution.py
@@ -246,7 +246,7 @@
 
     far_bits, near_bit = wide_bits[:-1], wide_bits[-1]
     far_steps = [("wide", bit) for bit in far_bits]
-    gathers = gathers_rows(total, clip_feats.shape[1])
+    gathers = len(far_bits) > 1 and gathers_rows(total, clip_feats.shape[1])
 
     block = jnp.concatenate(spread(teacher_text, far_steps), axis=0)
     across = swap(block, "wide", near_bit)
@@ -274,19 +274,38 @@
         )
 
     draw = loss_step(raw, teach_b, capt_all, place, total)
-    feats = spread(own_half(clip_feats, own_start, half), far_steps)
-    feats = [
-        jnp.concatenate(feats, axis=0),
-        swap(jnp.concatenate(feats[:-1], axis=0), "wide", near_bit),
-        swap(feats[-1], "wide", near_bit),
+    draws = [draw]
+    for index, bit in enumerate(far_bits):
+        prior = jnp.concatenate(draws, axis=0)
+        fresh = swap(prior, "wide", bit)
+        draws = [prior, fresh]
+        if not index:
+            first_step = fresh
+    across = swap(prior, "wide", near_bit)
+    last = swap(fresh, "wide", near_bit)
+    most = jnp.concatenate([prior, fresh, across], axis=0)
+    most = [most, swap(most, "mp", 1)]
+    rest = rows_of(last, draw, half)
+    last = [last, swap(last, "mp", 1)]
+
+    near = own_half(clip_feats, own_start, half)
+    near, moved = spread(near, [("wide", bit) for bit in reversed(far_bits)])
+    pairs = [
+        (near, moved),
+        (swap(near, "wide", near_bit), swap(moved, "wide", near_bit)),
     ]
+    pairs, _ = lax.optimization_barrier((pairs, first_step))
+    masks, turned = [0], [0]
+    for bit in far_bits:
+        masks += [mask ^ bit for mask in masks]
+    for bit in reversed(far_bits):
+        turned += [mask ^ bit for mask in turned]
+    feats = []
+    for pair in pairs:
+        blocks = [block for values in pair for block in jnp.split(values, len(masks) // 2)]
+        feats.append(jnp.concatenate([blocks[turned.index(mask)] for mask in masks], axis=0))
     feats.append(swap(jnp.concatenate(feats, axis=0), "mp", 1))
-    draws = spread(draw, far_steps)
-    across = swap(jnp.concatenate(draws[:-1], axis=0), "wide", near_bit)
-    last = swap(draws[-1], "wide", near_bit)
-    most = jnp.concatenate([*draws, across], axis=0)
-    most = [most, swap(most, "mp", 1)]
-    last = [last, swap(last, "mp", 1)]
+
     pre_t = jnp.concatenate(
         [
             lax.dot_general(
@@ -300,7 +319,6 @@
     slope_t = gelu_back(jnp.ones_like(pre_t))[0]
     hidden_t = gelu_t.astype(jnp.bfloat16)
     factors = (hidden_t, slope_t, stage(w_second))
-    rest = rows_of(last[0], draw, half)
     starts = [0, total // 2]
     last_starts = [total // 2 - rest, total - rest]
     sums = first_grads(most, starts, last_starts, feats, *factors, half)

time: 54.2 us -> 50.5 us (0.932)
  waiting for transfers between devices: 21.7 us -> 19.4 us
  starting transfers between devices: 21 us -> 19.2 us
  local copies, waits for them, and re-layouts: 1.72 us -> 2.36 us
    ppermute x20, waiting for transfers between devices: 21.7 us -> 19.4 us  [swap(): return lax.ppermute(values, axis, [(i, i ^ bit) for i in range(count)])]
    ppermute x20, starting transfers between devices: 21 us -> 19.2 us  [swap(): return lax.ppermute(values, axis, [(i, i ^ bit) for i in range(count)])]
    unnamed x19 -> x18, local copies, waits for them, and re-layouts: 1.59 us -> 2.14 us
    dot_general x4 -> x3, matrix products: 1.23 us -> 1.02 us  [body(): lax.dot_general(w_first, rows, (((0,), (1,)), ((), ())), preferred_elemen...]
  transfers between devices with their start and end apart: 20 -> 20, of which waited for: 8 -> 8; matrix products, arithmetic and copies ran while one was open for 10% -> 11% of each run, Pallas kernels for 4% -> 4%
where the time goes in v1:
time: 50.5 us; the launch traced here: 50.2 us
  waiting for transfers between devices  19.4 us (38%)
  starting transfers between devices  19.2 us (38%)
  Pallas kernels  3.29 us (7%)
  other arithmetic  2.58 us (5%)
  matrix products  2.46 us (5%)
  local copies, waits for them, and re-layouts  2.36 us (5%)
  between operations  1 us (2%)
    ppermute x20, waiting for transfers between devices, swap(): return lax.ppermute(values, axis, [(i, i ^ bit) for i in range(count)])  19.4 us
    ppermute x20, starting transfers between devices, swap(): return lax.ppermute(values, axis, [(i, i ^ bit) for i in range(count)])  19.2 us
    unnamed x18, local copies, waits for them, and re-layouts  2.14 us
    dot_general x1, matrix products, body(): raw = jnp.dot(hidden, w_second, preferred_element_type=jnp.float32)  1.44 us
    pallas_call x1, Pallas kernels, last_grads(): pl.pallas_call(kernel, out_shape=(jax.ShapeDtypeStruct((1, 1), jnp.float3...  1.39 us
    add_any x1, other arithmetic, gelu_exact(): return jax.nn.gelu(values, approximate=False)  1.17 us
    dot_general x3, matrix products, body(): lax.dot_general(w_first, rows, (((0,), (1,)), ((), ())), preferred_elemen...  1.02 us
  transfers between devices with their start and end apart: 20, of which 8 were waited for; matrix products, arithmetic and copies ran while one was open for 11% of the time, Pallas kernels for 4%

profile of v1, /device:TPU:0, one launch (start us, length us, event | category | flops | bytes accessed | tf_op | source)
XLA Modules:
  0.0 50.2 jit_solution(14330937748166900103)
XLA Ops:
  0.6 4.1 %collective-permute-start.2 = (bf16[32,512]{1,0:T(8,128)(2,1)}, bf16[32,512]{1,0:T(8,128)(2,1)S(1)}, u32[]{:S(2)}, u32[]{:S(2)}) collective-permute-start(bf16[32,512]{1,0:T(8,128)(2,1)} %param.8), channel_id=1, source_target_pairs={{0,16},{4,20},{8,24},{12,28},{16,0},{20,4},{24,8},{28,12},{1,17},{... | collective-permute-start | bytes 98312 | tf_op jit(solution)/shard_map/ppermute | solution.py:39
  4.8 1.4 %fusion.26 = f32[128,512]{1,0:T(8,128)S(1)} fusion(bf16[128,512]{1,0:T(8,128)(2,1)} %values_ref.1, bf16[128,768]{1,0:T(8,128)(2,1)} %param.6, bf16[768,128]{1,0:T(8,128)(2,1)S(1)} %copy-done), kind=kOutput, calls=%fused_computation.85 | convolution fusion | flops 43008000 | bytes 786432 | tf_op jit(solution)/shard_map/dot_general | solution.py:263
  6.3 0.8 %copy-done.4 = bf16[128,768]{1,0:T(8,128)(2,1)S(1)} copy-done((bf16[128,768]{1,0:T(8,128)(2,1)S(1)}, bf16[128,768]{1,0:T(8,128)(2,1)}, u32[]{:S(2)}) %copy-start.4) | copy-done | bytes 196632
  7.2 1.6 %collective-permute-start.13 = (bf16[64,768]{1,0:T(8,128)(2,1)S(1)}, bf16[64,768]{1,0:T(8,128)(2,1)S(1)}, u32[]{:S(2)}, u32[]{:S(2)}) collective-permute-start(bf16[64,768]{1,0:T(8,128)(2,1)S(1)} %constant_dynamic-slice_fusion), channel_id=1, source_target_pairs={{0,8},{4,12},{8,0},{12,4},{16,24},{20,28},{24,16},{28,20},{1,9},{5... | collective-permute-start | bytes 294920 | tf_op jit(solution)/shard_map/ppermute | solution.py:39
  9.0 0.7 %copy-done.3 = bf16[32,512]{1,0:T(8,128)(2,1)S(1)} copy-done((bf16[32,512]{1,0:T(8,128)(2,1)S(1)}, bf16[32,512]{1,0:T(8,128)(2,1)}, u32[]{:S(2)}) %copy-start.3) | copy-done | bytes 32792
  9.7 0.5 %collective-permute-start.3 = (bf16[64,512]{1,0:T(8,128)(2,1)S(1)}, bf16[64,512]{1,0:T(8,128)(2,1)S(1)}, u32[]{:S(2)}, u32[]{:S(2)}) collective-permute-start(bf16[64,512]{1,0:T(8,128)(2,1)S(1)} %pad_maximum_fusion.7), channel_id=1, source_target_pairs={{0,8},{4,12},{8,0},{12,4},{16,24},{20,28},{24,16},{28,20},{1,9},{5... | collective-permute-start | bytes 196616 | tf_op jit(solution)/shard_map/ppermute | solution.py:39
  10.2 3.8 %collective-permute-done.3 = bf16[64,512]{1,0:T(8,128)(2,1)S(1)} collective-permute-done((bf16[64,512]{1,0:T(8,128)(2,1)S(1)}, bf16[64,512]{1,0:T(8,128)(2,1)S(1)}, u32[]{:S(2)}, u32[]{:S(2)}) %collective-permute-start.3) | collective-permute-done | bytes 65568 | tf_op jit(solution)/shard_map/ppermute | solution.py:39
  14.2 1.6 %collective-permute-start.4 = (bf16[128,512]{1,0:T(8,128)(2,1)S(1)}, bf16[128,512]{1,0:T(8,128)(2,1)S(1)}, u32[]{:S(2)}, u32[]{:S(2)}) collective-permute-start(bf16[128,512]{1,0:T(8,128)(2,1)S(1)} %constant_dynamic-update-slice_fusion), channel_id=1, source_target_pairs={{0,2},{1,3},{2,0},{3,1},{4,6},{5,7},{6,4},{7,5},{8,10},{9,11},{10,... | collective-permute-start | bytes 393224 | tf_op jit(solution)/shard_map/ppermute | solution.py:39
  15.7 1.5 %collective-permute-start.5 = (bf16[128,512]{1,0:T(8,128)(2,1)S(1)}, bf16[128,512]{1,0:T(8,128)(2,1)S(1)}, u32[]{:S(2)}, u32[]{:S(2)}) collective-permute-start(bf16[128,512]{1,0:T(8,128)(2,1)S(1)} %constant_dynamic-update-slice_fusion), channel_id=1, source_target_pairs={{0,4},{4,0},{8,12},{12,8},{16,20},{20,16},{24,28},{28,24},{1,5},{5... | collective-permute-start | bytes 393224 | tf_op jit(solution)/shard_map/ppermute | solution.py:39
  17.4 0.9 %collective-permute-start.14 = (bf16[128,768]{1,0:T(8,128)(2,1)S(1)}, bf16[128,768]{1,0:T(8,128)(2,1)S(1)}, u32[]{:S(2)}, u32[]{:S(2)}) collective-permute-start(bf16[128,768]{1,0:T(8,128)(2,1)S(1)} %pad_maximum_fusion.5), channel_id=1, source_target_pairs={{0,16},{4,20},{8,24},{12,28},{16,0},{20,4},{24,8},{28,12},{1,17},{... | collective-permute-start | bytes 589832 | tf_op jit(solution)/shard_map/ppermute | solution.py:39
  18.3 0.6 %collective-permute-start.1 = (f32[64,512]{1,0:T(8,128)S(1)}, f32[64,512]{1,0:T(8,128)S(1)}, u32[]{:S(2)}, u32[]{:S(2)}) collective-permute-start(f32[64,512]{1,0:T(8,128)S(1)} %dynamic-slice_add_fusion), channel_id=1, source_target_pairs={{0,2},{1,3},{2,0},{3,1},{4,6},{5,7},{6,4},{7,5},{8,10},{9,11},{10,... | collective-permute-start | bytes 393224 | tf_op jit(solution)/shard_map/ppermute | solution.py:39
  18.9 0.9 %collective-permute-done.4 = bf16[128,512]{1,0:T(8,128)(2,1)S(1)} collective-permute-done((bf16[128,512]{1,0:T(8,128)(2,1)S(1)}, bf16[128,512]{1,0:T(8,128)(2,1)S(1)}, u32[]{:S(2)}, u32[]{:S(2)}) %collective-permute-start.4) | collective-permute-done | bytes 131104 | tf_op jit(solution)/shard_map/ppermute | solution.py:39
  20.0 0.7 %collective-permute-done.5 = bf16[128,512]{1,0:T(8,128)(2,1)S(1)} collective-permute-done((bf16[128,512]{1,0:T(8,128)(2,1)S(1)}, bf16[128,512]{1,0:T(8,128)(2,1)S(1)}, u32[]{:S(2)}, u32[]{:S(2)}) %collective-permute-start.5) | collective-permute-done | bytes 131104 | tf_op jit(solution)/shard_map/ppermute | solution.py:39
  20.8 1.6 %collective-permute-start.6 = (bf16[128,512]{1,0:T(8,128)(2,1)S(1)}, bf16[128,512]{1,0:T(8,128)(2,1)S(1)}, u32[]{:S(2)}, u32[]{:S(2)}) collective-permute-start(bf16[128,512]{1,0:T(8,128)(2,1)S(1)} %collective-permute-done.5), channel_id=1, source_target_pairs={{0,2},{1,3},{2,0},{3,1},{4,6},{5,7},{6,4},{7,5},{8,10},{9,11},{10,... | collective-permute-start | bytes 393224 | tf_op jit(solution)/shard_map/ppermute | solution.py:39
  22.7 3.1 %collective-permute-done.6 = bf16[128,512]{1,0:T(8,128)(2,1)S(1)} collective-permute-done((bf16[128,512]{1,0:T(8,128)(2,1)S(1)}, bf16[128,512]{1,0:T(8,128)(2,1)S(1)}, u32[]{:S(2)}, u32[]{:S(2)}) %collective-permute-start.6) | collective-permute-done | bytes 131104 | tf_op jit(solution)/shard_map/ppermute | solution.py:39
  26.2 0.6 %copy-done.5 = s32[128]{0:T(128)S(1)} copy-done((s32[128]{0:T(128)S(1)}, s32[128]{0:T(128)}, u32[]{:S(2)}) %copy-start.5) | copy-done | bytes 536
  26.9 1.5 %collective-permute-start.15 = (bf16[128,768]{1,0:T(8,128)(2,1)S(1)}, bf16[128,768]{1,0:T(8,128)(2,1)S(1)}, u32[]{:S(2)}, u32[]{:S(2)}) collective-permute-start(bf16[128,768]{1,0:T(8,128)(2,1)S(1)} %pad_maximum_fusion.5), channel_id=1, source_target_pairs={{0,4},{4,0},{8,12},{12,8},{16,20},{20,16},{24,28},{28,24},{1,5},{5... | collective-permute-start | bytes 589832 | tf_op jit(solution)/shard_map/ppermute | solution.py:39
  28.5 0.6 %collective-permute-start.16 = (bf16[128,768]{1,0:T(8,128)(2,1)S(1)}, bf16[128,768]{1,0:T(8,128)(2,1)S(1)}, u32[]{:S(2)}, u32[]{:S(2)}) collective-permute-start(bf16[128,768]{1,0:T(8,128)(2,1)S(1)} %collective-permute-done.14), channel_id=1, source_target_pairs={{0,4},{4,0},{8,12},{12,8},{16,20},{20,16},{24,28},{28,24},{1,5},{5... | collective-permute-start | bytes 589832 | tf_op jit(solution)/shard_map/ppermute | solution.py:39
  29.2 1.0 %loss_step.1 = bf16[264,128]{1,0:T(8,128)(2,1)S(1)} custom-call(f32[64,512]{1,0:T(8,128)S(1)} %add.119.raw_ref, bf16[64,512]{1,0:T(8,128)(2,1)S(1)} %fusion.15.teach_ref, bf16[1024,512]{1,0:T(8,128)(2,1)S(1)} %constant_dynamic-update-slice_fusion.3.capt_ref, s32[64,1]{1,0:T(8,128)S(1)} %copy.9.place_ref), custom_call_target="tpu_custom_call" | custom-call | tf_op jit(solution)/shard_map/loss_step/pallas_call | solution.py:99
  30.1 1.1 %collective-permute-start.9 = (bf16[264,128]{1,0:T(8,128)(2,1)S(1)}, bf16[264,128]{1,0:T(8,128)(2,1)S(1)}, u32[]{:S(2)}, u32[]{:S(2)}) collective-permute-start(bf16[264,128]{1,0:T(8,128)(2,1)S(1)} %loss_step.1), channel_id=1, source_target_pairs={{0,16},{4,20},{8,24},{12,28},{16,0},{20,4},{24,8},{28,12},{1,17},{... | collective-permute-start | bytes 202760 | tf_op jit(solution)/shard_map/ppermute | solution.py:39
  31.2 4.9 %collective-permute-done.9 = bf16[264,128]{1,0:T(8,128)(2,1)S(1)} collective-permute-done((bf16[264,128]{1,0:T(8,128)(2,1)S(1)}, bf16[264,128]{1,0:T(8,128)(2,1)S(1)}, u32[]{:S(2)}, u32[]{:S(2)}) %collective-permute-start.9) | collective-permute-done | bytes 67616 | tf_op jit(solution)/shard_map/ppermute | solution.py:39
  36.2 1.6 %collective-permute-start.18 = (bf16[528,128]{1,0:T(8,128)(2,1)S(1)}, bf16[528,128]{1,0:T(8,128)(2,1)S(1)}, u32[]{:S(2)}, u32[]{:S(2)}) collective-permute-start(bf16[528,128]{1,0:T(8,128)(2,1)S(1)} %pad_maximum_fusion.6), channel_id=1, source_target_pairs={{0,4},{4,0},{8,12},{12,8},{16,20},{20,16},{24,28},{28,24},{1,5},{5... | collective-permute-start | bytes 405512 | tf_op jit(solution)/shard_map/ppermute | solution.py:39
  37.8 0.9 %collective-permute-done.16 = bf16[128,768]{1,0:T(8,128)(2,1)S(1)} collective-permute-done((bf16[128,768]{1,0:T(8,128)(2,1)S(1)}, bf16[128,768]{1,0:T(8,128)(2,1)S(1)}, u32[]{:S(2)}, u32[]{:S(2)}) %collective-permute-start.16) | collective-permute-done | bytes 196640 | tf_op jit(solution)/shard_map/ppermute | solution.py:39
  39.0 0.3 convolution_bitcast_fusion.2
  39.3 0.3 convolution_bitcast_fusion.1
  39.7 1.5 %collective-permute-done.10 = bf16[528,128]{1,0:T(8,128)(2,1)S(1)} collective-permute-done((bf16[528,128]{1,0:T(8,128)(2,1)S(1)}, bf16[528,128]{1,0:T(8,128)(2,1)S(1)}, u32[]{:S(2)}, u32[]{:S(2)}) %collective-permute-start.10) | collective-permute-done | bytes 135200 | tf_op jit(solution)/shard_map/ppermute | solution.py:39
  41.2 1.5 %collective-permute-start.11 = (bf16[528,128]{1,0:T(8,128)(2,1)S(1)}, bf16[528,128]{1,0:T(8,128)(2,1)S(1)}, u32[]{:S(2)}, u32[]{:S(2)}) collective-permute-start(bf16[528,128]{1,0:T(8,128)(2,1)S(1)} %collective-permute-done.10), channel_id=1, source_target_pairs={{0,4},{4,0},{8,12},{12,8},{16,20},{20,16},{24,28},{28,24},{1,5},{5... | collective-permute-start | bytes 405512 | tf_op jit(solution)/shard_map/ppermute | solution.py:39
  42.8 3.4 %collective-permute-done.11.refs_0_ = bf16[528,128]{1,0:T(8,128)(2,1)S(1)} collective-permute-done((bf16[528,128]{1,0:T(8,128)(2,1)S(1)}, bf16[528,128]{1,0:T(8,128)(2,1)S(1)}, u32[]{:S(2)}, u32[]{:S(2)}) %collective-permute-start.11) | collective-permute-done | bytes 135200 | tf_op jit(solution)/shard_map/ppermute | solution.py:39
  46.2 0.4 convolution_bitcast_fusion
  46.6 1.2 %multiply_add_fusion = (f32[128,1024]{1,0:T(8,128)S(1)}, f32[128,1024]{1,0:T(8,128)S(1)}) fusion(f32[128,512]{1,0:T(8,128)S(1)} %convolution_bitcast_fusion, f32[128,256]{1,0:T(8,128)S(1)} %convolution_bitcast_fusion.1, f32[128,256]{1,0:T(8,128)S(1)} %convolution_bitcast_fusion.2), kind=kLoop, calls=%fused_computation.6 | loop fusion | flops 9175040 | bytes 1572864 | tf_op jit(solution)/shard_map/transpose(jvp())/add_any | solution.py:233
  47.9 0.9 %first_grads.1 = (f32[768,128]{1,0:T(8,128)S(1)}, f32[128,512]{1,0:T(8,128)S(1)}, f32[8,128]{1,0:T(8,128)S(1)}, bf16[768,256]{1,0:T(8,128)(2,1)S(1)}) custom-call(bf16[1584,128]{1,0:T(8,128)(2,1)S(1)} %pad_maximum_fusion.1.refs_0_, bf16[1584,128]{1,0:T(8,128)(2,1)S(1)} %collective-permute-done.19.refs_1_, bf16[256,768]{1,0:T(8,128)(2,1)S(1)} %get-tuple-element.47.refs_2_, ...), custom_call_target="tpu_custom_call" | custom-call | tf_op jit(solution)/shard_map/first_grads/pallas_call | solution.py:166
  48.8 1.4 %last_grads.1 = (f32[1,1]{1,0:T(1,128)}, f32[768,128]{1,0:T(8,128)}, f32[128,512]{1,0:T(8,128)}) custom-call(bf16[528,128]{1,0:T(8,128)(2,1)S(1)} %collective-permute-done.11.refs_0_, bf16[528,128]{1,0:T(8,128)(2,1)S(1)} %collective-permute-done.12.refs_1_, bf16[128,1024]{1,0:T(8,128)(2,1)S(1)} %multiply_convert_fusion.refs_5_.refs_2_, ...), custom_call_target="tpu_custom_call" | custom-call | tf_op jit(solution)/shard_map/last_grads/pallas_call | solution.py:204
  (70 shorter events, 2.2 us)
Async XLA Ops:
  0.6 4.1 %copy-start = (bf16[768,128]{1,0:T(8,128)(2,1)S(1)}, bf16[768,128]{1,0:T(8,128)(2,1)}, u32[]{:S(2)}) copy-start(bf16[768,128]{1,0:T(8,128)(2,1)} %param.9) | copy-start | bytes 589828
  0.6 9.1 %collective-permute-start.2 = (bf16[32,512]{1,0:T(8,128)(2,1)}, bf16[32,512]{1,0:T(8,128)(2,1)S(1)}, u32[]{:S(2)}, u32[]{:S(2)}) collective-permute-start(bf16[32,512]{1,0:T(8,128)(2,1)} %param.8), channel_id=1, source_target_pairs={{0,16},{4,20},{8,24},{12,28},{16,0},{20,4},{24,8},{28,12},{1,17},{... | collective-permute-start | bytes 98312 | tf_op jit(solution)/shard_map/ppermute | solution.py:39
  6.2 0.9 %copy-start.4 = (bf16[128,768]{1,0:T(8,128)(2,1)S(1)}, bf16[128,768]{1,0:T(8,128)(2,1)}, u32[]{:S(2)}) copy-start(bf16[128,768]{1,0:T(8,128)(2,1)} %param.6) | copy-start | bytes 589828
  6.2 2.6 %copy-start.2 = (bf16[128,512]{1,0:T(8,128)(2,1)S(1)}, bf16[128,512]{1,0:T(8,128)(2,1)}, u32[]{:S(2)}) copy-start(bf16[128,512]{1,0:T(8,128)(2,1)} %param.7) | copy-start | bytes 393220
  6.3 12.0 %collective-permute-start = (f32[64,512]{1,0:T(8,128)S(1)}, f32[64,512]{1,0:T(8,128)S(1)}, u32[]{:S(2)}, u32[]{:S(2)}) collective-permute-start(f32[64,512]{1,0:T(8,128)S(1)} %constant_dynamic-slice_fusion.1), channel_id=1, source_target_pairs={{0,1},{1,0},{2,3},{3,2},{4,5},{5,4},{6,7},{7,6},{8,9},{9,8},{10,11... | collective-permute-start | bytes 393224 | tf_op jit(solution)/shard_map/ppermute | solution.py:39
  7.2 10.2 %collective-permute-start.13 = (bf16[64,768]{1,0:T(8,128)(2,1)S(1)}, bf16[64,768]{1,0:T(8,128)(2,1)S(1)}, u32[]{:S(2)}, u32[]{:S(2)}) collective-permute-start(bf16[64,768]{1,0:T(8,128)(2,1)S(1)} %constant_dynamic-slice_fusion), channel_id=1, source_target_pairs={{0,8},{4,12},{8,0},{12,4},{16,24},{20,28},{24,16},{28,20},{1,9},{5... | collective-permute-start | bytes 294920 | tf_op jit(solution)/shard_map/ppermute | solution.py:39
  8.9 0.8 %copy-start.3 = (bf16[32,512]{1,0:T(8,128)(2,1)S(1)}, bf16[32,512]{1,0:T(8,128)(2,1)}, u32[]{:S(2)}) copy-start(bf16[32,512]{1,0:T(8,128)(2,1)} %param.8) | copy-start | bytes 98308
  9.7 4.3 %collective-permute-start.3 = (bf16[64,512]{1,0:T(8,128)(2,1)S(1)}, bf16[64,512]{1,0:T(8,128)(2,1)S(1)}, u32[]{:S(2)}, u32[]{:S(2)}) collective-permute-start(bf16[64,512]{1,0:T(8,128)(2,1)S(1)} %pad_maximum_fusion.7), channel_id=1, source_target_pairs={{0,8},{4,12},{8,0},{12,4},{16,24},{20,28},{24,16},{28,20},{1,9},{5... | collective-permute-start | bytes 196616 | tf_op jit(solution)/shard_map/ppermute | solution.py:39
  14.2 5.7 %collective-permute-start.4 = (bf16[128,512]{1,0:T(8,128)(2,1)S(1)}, bf16[128,512]{1,0:T(8,128)(2,1)S(1)}, u32[]{:S(2)}, u32[]{:S(2)}) collective-permute-start(bf16[128,512]{1,0:T(8,128)(2,1)S(1)} %constant_dynamic-update-slice_fusion), channel_id=1, source_target_pairs={{0,2},{1,3},{2,0},{3,1},{4,6},{5,7},{6,4},{7,5},{8,10},{9,11},{10,... | collective-permute-start | bytes 393224 | tf_op jit(solution)/shard_map/ppermute | solution.py:39
  15.7 5.0 %collective-permute-start.5 = (bf16[128,512]{1,0:T(8,128)(2,1)S(1)}, bf16[128,512]{1,0:T(8,128)(2,1)S(1)}, u32[]{:S(2)}, u32[]{:S(2)}) collective-permute-start(bf16[128,512]{1,0:T(8,128)(2,1)S(1)} %constant_dynamic-update-slice_fusion), channel_id=1, source_target_pairs={{0,4},{4,0},{8,12},{12,8},{16,20},{20,16},{24,28},{28,24},{1,5},{5... | collective-permute-start | bytes 393224 | tf_op jit(solution)/shard_map/ppermute | solution.py:39
  17.4 11.1 %collective-permute-start.14 = (bf16[128,768]{1,0:T(8,128)(2,1)S(1)}, bf16[128,768]{1,0:T(8,128)(2,1)S(1)}, u32[]{:S(2)}, u32[]{:S(2)}) collective-permute-start(bf16[128,768]{1,0:T(8,128)(2,1)S(1)} %pad_maximum_fusion.5), channel_id=1, source_target_pairs={{0,16},{4,20},{8,24},{12,28},{16,0},{20,4},{24,8},{28,12},{1,17},{... | collective-permute-start | bytes 589832 | tf_op jit(solution)/shard_map/ppermute | solution.py:39
  18.3 10.2 %collective-permute-start.1 = (f32[64,512]{1,0:T(8,128)S(1)}, f32[64,512]{1,0:T(8,128)S(1)}, u32[]{:S(2)}, u32[]{:S(2)}) collective-permute-start(f32[64,512]{1,0:T(8,128)S(1)} %dynamic-slice_add_fusion), channel_id=1, source_target_pairs={{0,2},{1,3},{2,0},{3,1},{4,6},{5,7},{6,4},{7,5},{8,10},{9,11},{10,... | collective-permute-start | bytes 393224 | tf_op jit(solution)/shard_map/ppermute | solution.py:39
  20.8 5.0 %collective-permute-start.6 = (bf16[128,512]{1,0:T(8,128)(2,1)S(1)}, bf16[128,512]{1,0:T(8,128)(2,1)S(1)}, u32[]{:S(2)}, u32[]{:S(2)}) collective-permute-start(bf16[128,512]{1,0:T(8,128)(2,1)S(1)} %collective-permute-done.5), channel_id=1, source_target_pairs={{0,2},{1,3},{2,0},{3,1},{4,6},{5,7},{6,4},{7,5},{8,10},{9,11},{10,... | collective-permute-start | bytes 393224 | tf_op jit(solution)/shard_map/ppermute | solution.py:39
  22.6 6.5 %collective-permute-start.7 = (bf16[384,512]{1,0:T(8,128)(2,1)S(1)}, bf16[384,512]{1,0:T(8,128)(2,1)S(1)}, u32[]{:S(2)}, u32[]{:S(2)}) collective-permute-start(bf16[384,512]{1,0:T(8,128)(2,1)S(1)} %pad_maximum_fusion.2), channel_id=1, source_target_pairs={{0,1},{1,0},{2,3},{3,2},{4,5},{5,4},{6,7},{7,6},{8,9},{9,8},{10,11... | collective-permute-start | bytes 1179656 | tf_op jit(solution)/shard_map/ppermute | solution.py:39
  26.1 0.7 %copy-start.5 = (s32[128]{0:T(128)S(1)}, s32[128]{0:T(128)}, u32[]{:S(2)}) copy-start(s32[128]{0:T(128)} %param.11) | copy-start | bytes 1540
  26.1 3.0 %collective-permute-start.8 = (bf16[128,512]{1,0:T(8,128)(2,1)S(1)}, bf16[128,512]{1,0:T(8,128)(2,1)S(1)}, u32[]{:S(2)}, u32[]{:S(2)}) collective-permute-start(bf16[128,512]{1,0:T(8,128)(2,1)S(1)} %get-tuple-element.28), channel_id=1, source_target_pairs={{0,1},{1,0},{2,3},{3,2},{4,5},{5,4},{6,7},{7,6},{8,9},{9,8},{10,11... | collective-permute-start | bytes 393224 | tf_op jit(solution)/shard_map/ppermute | solution.py:39
  26.9 10.9 %collective-permute-start.15 = (bf16[128,768]{1,0:T(8,128)(2,1)S(1)}, bf16[128,768]{1,0:T(8,128)(2,1)S(1)}, u32[]{:S(2)}, u32[]{:S(2)}) collective-permute-start(bf16[128,768]{1,0:T(8,128)(2,1)S(1)} %pad_maximum_fusion.5), channel_id=1, source_target_pairs={{0,4},{4,0},{8,12},{12,8},{16,20},{20,16},{24,28},{28,24},{1,5},{5... | collective-permute-start | bytes 589832 | tf_op jit(solution)/shard_map/ppermute | solution.py:39
  28.5 10.2 %collective-permute-start.16 = (bf16[128,768]{1,0:T(8,128)(2,1)S(1)}, bf16[128,768]{1,0:T(8,128)(2,1)S(1)}, u32[]{:S(2)}, u32[]{:S(2)}) collective-permute-start(bf16[128,768]{1,0:T(8,128)(2,1)S(1)} %collective-permute-done.14), channel_id=1, source_target_pairs={{0,4},{4,0},{8,12},{12,8},{16,20},{20,16},{24,28},{28,24},{1,5},{5... | collective-permute-start | bytes 589832 | tf_op jit(solution)/shard_map/ppermute | solution.py:39
  29.2 2.0 %copy-start.1 = (bf16[128,512]{1,0:T(8,128)(2,1)S(1)}, bf16[128,512]{1,0:T(8,128)(2,1)}, u32[]{:S(2)}) copy-start(bf16[128,512]{1,0:T(8,128)(2,1)} %values_ref.1) | copy-start | bytes 393220
  30.1 6.0 %collective-permute-start.9 = (bf16[264,128]{1,0:T(8,128)(2,1)S(1)}, bf16[264,128]{1,0:T(8,128)(2,1)S(1)}, u32[]{:S(2)}, u32[]{:S(2)}) collective-permute-start(bf16[264,128]{1,0:T(8,128)(2,1)S(1)} %loss_step.1), channel_id=1, source_target_pairs={{0,16},{4,20},{8,24},{12,28},{16,0},{20,4},{24,8},{28,12},{1,17},{... | collective-permute-start | bytes 202760 | tf_op jit(solution)/shard_map/ppermute | solution.py:39
  36.1 5.1 %collective-permute-start.10 = (bf16[528,128]{1,0:T(8,128)(2,1)S(1)}, bf16[528,128]{1,0:T(8,128)(2,1)S(1)}, u32[]{:S(2)}, u32[]{:S(2)}) collective-permute-start(bf16[528,128]{1,0:T(8,128)(2,1)S(1)} %pad_maximum_fusion.6), channel_id=1, source_target_pairs={{0,8},{4,12},{8,0},{12,4},{16,24},{20,28},{24,16},{28,20},{1,9},{5... | collective-permute-start | bytes 405512 | tf_op jit(solution)/shard_map/ppermute | solution.py:39
  36.2 6.5 %collective-permute-start.18 = (bf16[528,128]{1,0:T(8,128)(2,1)S(1)}, bf16[528,128]{1,0:T(8,128)(2,1)S(1)}, u32[]{:S(2)}, u32[]{:S(2)}) collective-permute-start(bf16[528,128]{1,0:T(8,128)(2,1)S(1)} %pad_maximum_fusion.6), channel_id=1, source_target_pairs={{0,4},{4,0},{8,12},{12,8},{16,20},{20,16},{24,28},{28,24},{1,5},{5... | collective-permute-start | bytes 405512 | tf_op jit(solution)/shard_map/ppermute | solution.py:39
  38.9 7.3 %collective-permute-start.17 = (bf16[512,768]{1,0:T(8,128)(2,1)S(1)}, bf16[512,768]{1,0:T(8,128)(2,1)S(1)}, u32[]{:S(2)}, u32[]{:S(2)}) collective-permute-start(bf16[512,768]{1,0:T(8,128)(2,1)S(1)} %constant_dynamic-update-slice_fusion.9), channel_id=1, source_target_pairs={{0,1},{1,0},{2,3},{3,2},{4,5},{5,4},{6,7},{7,6},{8,9},{9,8},{10,11... | collective-permute-start | bytes 2359304 | tf_op jit(solution)/shard_map/ppermute | solution.py:39
  41.2 5.0 %collective-permute-start.11 = (bf16[528,128]{1,0:T(8,128)(2,1)S(1)}, bf16[528,128]{1,0:T(8,128)(2,1)S(1)}, u32[]{:S(2)}, u32[]{:S(2)}) collective-permute-start(bf16[528,128]{1,0:T(8,128)(2,1)S(1)} %collective-permute-done.10), channel_id=1, source_target_pairs={{0,4},{4,0},{8,12},{12,8},{16,20},{20,16},{24,28},{28,24},{1,5},{5... | collective-permute-start | bytes 405512 | tf_op jit(solution)/shard_map/ppermute | solution.py:39
  42.8 5.1 %collective-permute-start.19 = (bf16[1584,128]{1,0:T(8,128)(2,1)S(1)}, bf16[1584,128]{1,0:T(8,128)(2,1)S(1)}, u32[]{:S(2)}, u32[]{:S(2)}) collective-permute-start(bf16[1584,128]{1,0:T(8,128)(2,1)S(1)} %pad_maximum_fusion.1.refs_0_), channel_id=1, source_target_pairs={{0,1},{1,0},{2,3},{3,2},{4,5},{5,4},{6,7},{7,6},{8,9},{9,8},{10,11... | collective-permute-start | bytes 1216520 | tf_op jit(solution)/shard_map/ppermute | solution.py:39
  46.2 2.6 %collective-permute-start.12 = (bf16[528,128]{1,0:T(8,128)(2,1)S(1)}, bf16[528,128]{1,0:T(8,128)(2,1)S(1)}, u32[]{:S(2)}, u32[]{:S(2)}) collective-permute-start(bf16[528,128]{1,0:T(8,128)(2,1)S(1)} %collective-permute-done.11.refs_0_), channel_id=1, source_target_pairs={{0,1},{1,0},{2,3},{3,2},{4,5},{5,4},{6,7},{7,6},{8,9},{9,8},{10,11... | collective-permute-start | bytes 405512 | tf_op jit(solution)/shard_map/ppermute | solution.py:39

commit v2 on v1

--- a/solution.py
+++ b/solution.py
@@ -274,13 +274,17 @@
         )
 
     draw = loss_step(raw, teach_b, capt_all, place, total)
-    draws = [draw]
-    for index, bit in enumerate(far_bits):
-        prior = jnp.concatenate(draws, axis=0)
-        fresh = swap(prior, "wide", bit)
-        draws = [prior, fresh]
-        if not index:
-            first_step = fresh
+    sent, masks = [0], [0]
+    for bit in far_bits:
+        sent += [mask ^ bit for mask in sent]
+    for bit in reversed(far_bits):
+        masks += [mask ^ bit for mask in masks]
+    draws = {0: draw}
+    for mask in sent[1:]:
+        draws[mask] = swap(draw, "wide", mask)
+    middle = len(masks) // 2
+    prior = jnp.concatenate([draws[mask] for mask in masks[:middle]], axis=0)
+    fresh = jnp.concatenate([draws[mask] for mask in masks[middle:]], axis=0)
     across = swap(prior, "wide", near_bit)
     last = swap(fresh, "wide", near_bit)
     most = jnp.concatenate([prior, fresh, across], axis=0)
@@ -294,16 +298,8 @@
         (near, moved),
         (swap(near, "wide", near_bit), swap(moved, "wide", near_bit)),
     ]
-    pairs, _ = lax.optimization_barrier((pairs, first_step))
-    masks, turned = [0], [0]
-    for bit in far_bits:
-        masks += [mask ^ bit for mask in masks]
-    for bit in reversed(far_bits):
-        turned += [mask ^ bit for mask in turned]
-    feats = []
-    for pair in pairs:
-        blocks = [block for values in pair for block in jnp.split(values, len(masks) // 2)]
-        feats.append(jnp.concatenate([blocks[turned.index(mask)] for mask in masks], axis=0))
+    pairs = [lax.optimization_barrier((*pair, draws[masks[1]]))[:2] for pair in pairs]
+    feats = [jnp.concatenate(pair, axis=0) for pair in pairs]
     feats.append(swap(jnp.concatenate(feats, axis=0), "mp", 1))
 
     pre_t = jnp.concatenate(

time: 50.5 us -> 48.2 us (0.954)
  waiting for transfers between devices: 19.4 us -> 16.6 us
  starting transfers between devices: 19.2 us -> 21.7 us
  local copies, waits for them, and re-layouts: 2.36 us -> 0.32 us
    ppermute x20 -> x21, waiting for transfers between devices: 19.4 us -> 16.6 us  [swap(): return lax.ppermute(values, axis, [(i, i ^ bit) for i in range(count)])]
    ppermute x20 -> x21, starting transfers between devices: 19.2 us -> 21.7 us  [swap(): return lax.ppermute(values, axis, [(i, i ^ bit) for i in range(count)])]
    unnamed x18 -> x21, local copies, waits for them, and re-layouts: 2.14 us -> 0.14 us
  transfers between devices with their start and end apart: 20 -> 21, of which waited for: 8 -> 8; matrix products, arithmetic and copies ran while one was open for 11% -> 11% of each run, Pallas kernels for 4% -> 4%
where the time goes in v2:
time: 48.2 us; the launch traced here: 48 us
  starting transfers between devices  21.7 us (45%)
  waiting for transfers between devices  16.6 us (34%)
  Pallas kernels  3.3 us (7%)
  other arithmetic  2.57 us (5%)
  matrix products  2.5 us (5%)
  between operations  1.03 us (2%)
    ppermute x21, starting transfers between devices, swap(): return lax.ppermute(values, axis, [(i, i ^ bit) for i in range(count)])  21.7 us
    ppermute x21, waiting for transfers between devices, swap(): return lax.ppermute(values, axis, [(i, i ^ bit) for i in range(count)])  16.6 us
    dot_general x1, matrix products, body(): raw = jnp.dot(hidden, w_second, preferred_element_type=jnp.float32)  1.49 us
    pallas_call x1, Pallas kernels, last_grads(): pl.pallas_call(kernel, out_shape=(jax.ShapeDtypeStruct((1, 1), jnp.float3...  1.39 us
    add_any x1, other arithmetic, gelu_exact(): return jax.nn.gelu(values, approximate=False)  1.17 us
    dot_general x3, matrix products, body(): lax.dot_general(w_first, rows, (((0,), (1,)), ((), ())), preferred_elemen...  1.01 us
    pallas_call x1, Pallas kernels, loss_step(): pl.pallas_call(kernel, out_shape=jax.ShapeDtypeStruct((rows * width // la...  0.97 us
  transfers between devices with their start and end apart: 21, of which 8 were waited for; matrix products, arithmetic and copies ran while one was open for 11% of the time, Pallas kernels for 4%

profile of v2, /device:TPU:0, one launch (start us, length us, event | category | flops | bytes accessed | tf_op | source)
XLA Modules:
  0.0 48.0 jit_solution(7483860050574657430)
XLA Ops:
  0.6 4.1 %collective-permute-start.2 = (bf16[32,512]{1,0:T(8,128)(2,1)}, bf16[32,512]{1,0:T(8,128)(2,1)S(1)}, u32[]{:S(2)}, u32[]{:S(2)}) collective-permute-start(bf16[32,512]{1,0:T(8,128)(2,1)} %param.8), channel_id=1, source_target_pairs={{0,16},{4,20},{8,24},{12,28},{16,0},{20,4},{24,8},{28,12},{1,17},{... | collective-permute-start | bytes 98312 | tf_op jit(solution)/shard_map/ppermute | solution.py:39
  4.8 1.5 %fusion.26 = f32[128,512]{1,0:T(8,128)S(1)} fusion(bf16[128,512]{1,0:T(8,128)(2,1)} %values_ref.1, bf16[128,768]{1,0:T(8,128)(2,1)} %param.6, bf16[768,128]{1,0:T(8,128)(2,1)S(1)} %copy-done), kind=kOutput, calls=%fused_computation.85 | convolution fusion | flops 43008000 | bytes 786432 | tf_op jit(solution)/shard_map/dot_general | solution.py:263
  6.4 1.6 %collective-permute-start.13 = (bf16[64,768]{1,0:T(8,128)(2,1)S(1)}, bf16[64,768]{1,0:T(8,128)(2,1)S(1)}, u32[]{:S(2)}, u32[]{:S(2)}) collective-permute-start(bf16[64,768]{1,0:T(8,128)(2,1)S(1)} %constant_dynamic-slice_fusion), channel_id=1, source_target_pairs={{0,8},{4,12},{8,0},{12,4},{16,24},{20,28},{24,16},{28,20},{1,9},{5... | collective-permute-start | bytes 294920 | tf_op jit(solution)/shard_map/ppermute | solution.py:39
  8.3 0.5 %collective-permute-start.3 = (bf16[64,512]{1,0:T(8,128)(2,1)S(1)}, bf16[64,512]{1,0:T(8,128)(2,1)S(1)}, u32[]{:S(2)}, u32[]{:S(2)}) collective-permute-start(bf16[64,512]{1,0:T(8,128)(2,1)S(1)} %pad_maximum_fusion.6), channel_id=1, source_target_pairs={{0,8},{4,12},{8,0},{12,4},{16,24},{20,28},{24,16},{28,20},{1,9},{5... | collective-permute-start | bytes 196616 | tf_op jit(solution)/shard_map/ppermute | solution.py:39
  8.9 4.2 %collective-permute-done.3 = bf16[64,512]{1,0:T(8,128)(2,1)S(1)} collective-permute-done((bf16[64,512]{1,0:T(8,128)(2,1)S(1)}, bf16[64,512]{1,0:T(8,128)(2,1)S(1)}, u32[]{:S(2)}, u32[]{:S(2)}) %collective-permute-start.3) | collective-permute-done | bytes 65568 | tf_op jit(solution)/shard_map/ppermute | solution.py:39
  13.2 1.6 %collective-permute-start.4 = (bf16[128,512]{1,0:T(8,128)(2,1)S(1)}, bf16[128,512]{1,0:T(8,128)(2,1)S(1)}, u32[]{:S(2)}, u32[]{:S(2)}) collective-permute-start(bf16[128,512]{1,0:T(8,128)(2,1)S(1)} %constant_dynamic-update-slice_fusion), channel_id=1, source_target_pairs={{0,2},{1,3},{2,0},{3,1},{4,6},{5,7},{6,4},{7,5},{8,10},{9,11},{10,... | collective-permute-start | bytes 393224 | tf_op jit(solution)/shard_map/ppermute | solution.py:39
  14.7 1.5 %collective-permute-start.5 = (bf16[128,512]{1,0:T(8,128)(2,1)S(1)}, bf16[128,512]{1,0:T(8,128)(2,1)S(1)}, u32[]{:S(2)}, u32[]{:S(2)}) collective-permute-start(bf16[128,512]{1,0:T(8,128)(2,1)S(1)} %constant_dynamic-update-slice_fusion), channel_id=1, source_target_pairs={{0,4},{4,0},{8,12},{12,8},{16,20},{20,16},{24,28},{28,24},{1,5},{5... | collective-permute-start | bytes 393224 | tf_op jit(solution)/shard_map/ppermute | solution.py:39
  16.4 1.1 %collective-permute-start.14 = (bf16[128,768]{1,0:T(8,128)(2,1)S(1)}, bf16[128,768]{1,0:T(8,128)(2,1)S(1)}, u32[]{:S(2)}, u32[]{:S(2)}) collective-permute-start(bf16[128,768]{1,0:T(8,128)(2,1)S(1)} %pad_maximum_fusion.3), channel_id=1, source_target_pairs={{0,16},{4,20},{8,24},{12,28},{16,0},{20,4},{24,8},{28,12},{1,17},{... | collective-permute-start | bytes 589832 | tf_op jit(solution)/shard_map/ppermute | solution.py:39
  17.5 0.6 %collective-permute-start.1 = (f32[64,512]{1,0:T(8,128)S(1)}, f32[64,512]{1,0:T(8,128)S(1)}, u32[]{:S(2)}, u32[]{:S(2)}) collective-permute-start(f32[64,512]{1,0:T(8,128)S(1)} %dynamic-slice_add_fusion), channel_id=1, source_target_pairs={{0,2},{1,3},{2,0},{3,1},{4,6},{5,7},{6,4},{7,5},{8,10},{9,11},{10,... | collective-permute-start | bytes 393224 | tf_op jit(solution)/shard_map/ppermute | solution.py:39
  18.1 0.2 collective-permute-done.4
  18.4 1.3 %collective-permute-done.5 = bf16[128,512]{1,0:T(8,128)(2,1)S(1)} collective-permute-done((bf16[128,512]{1,0:T(8,128)(2,1)S(1)}, bf16[128,512]{1,0:T(8,128)(2,1)S(1)}, u32[]{:S(2)}, u32[]{:S(2)}) %collective-permute-start.5) | collective-permute-done | bytes 131104 | tf_op jit(solution)/shard_map/ppermute | solution.py:39
  19.8 1.2 %collective-permute-start.6 = (bf16[128,512]{1,0:T(8,128)(2,1)S(1)}, bf16[128,512]{1,0:T(8,128)(2,1)S(1)}, u32[]{:S(2)}, u32[]{:S(2)}) collective-permute-start(bf16[128,512]{1,0:T(8,128)(2,1)S(1)} %collective-permute-done.5), channel_id=1, source_target_pairs={{0,2},{1,3},{2,0},{3,1},{4,6},{5,7},{6,4},{7,5},{8,10},{9,11},{10,... | collective-permute-start | bytes 393224 | tf_op jit(solution)/shard_map/ppermute | solution.py:39
  21.3 3.9 %collective-permute-done.6 = bf16[128,512]{1,0:T(8,128)(2,1)S(1)} collective-permute-done((bf16[128,512]{1,0:T(8,128)(2,1)S(1)}, bf16[128,512]{1,0:T(8,128)(2,1)S(1)}, u32[]{:S(2)}, u32[]{:S(2)}) %collective-permute-start.6) | collective-permute-done | bytes 131104 | tf_op jit(solution)/shard_map/ppermute | solution.py:39
  25.5 0.1 fusion.73
  25.8 1.2 %collective-permute-start.16 = (bf16[128,768]{1,0:T(8,128)(2,1)S(1)}, bf16[128,768]{1,0:T(8,128)(2,1)S(1)}, u32[]{:S(2)}, u32[]{:S(2)}) collective-permute-start(bf16[128,768]{1,0:T(8,128)(2,1)S(1)} %pad_maximum_fusion.3), channel_id=1, source_target_pairs={{0,4},{4,0},{8,12},{12,8},{16,20},{20,16},{24,28},{28,24},{1,5},{5... | collective-permute-start | bytes 589832 | tf_op jit(solution)/shard_map/ppermute | solution.py:39
  27.0 0.5 %collective-permute-done.14 = bf16[128,768]{1,0:T(8,128)(2,1)S(1)} collective-permute-done((bf16[128,768]{1,0:T(8,128)(2,1)S(1)}, bf16[128,768]{1,0:T(8,128)(2,1)S(1)}, u32[]{:S(2)}, u32[]{:S(2)}) %collective-permute-start.14) | collective-permute-done | bytes 196640 | tf_op jit(solution)/shard_map/ppermute | solution.py:39
  27.5 0.5 %collective-permute-start.17 = (bf16[128,768]{1,0:T(8,128)(2,1)S(1)}, bf16[128,768]{1,0:T(8,128)(2,1)S(1)}, u32[]{:S(2)}, u32[]{:S(2)}) collective-permute-start(bf16[128,768]{1,0:T(8,128)(2,1)S(1)} %collective-permute-done.14), channel_id=1, source_target_pairs={{0,4},{4,0},{8,12},{12,8},{16,20},{20,16},{24,28},{28,24},{1,5},{5... | collective-permute-start | bytes 589832 | tf_op jit(solution)/shard_map/ppermute | solution.py:39
  28.0 1.0 %loss_step.1 = bf16[264,128]{1,0:T(8,128)(2,1)S(1)} custom-call(f32[64,512]{1,0:T(8,128)S(1)} %add.119.raw_ref, bf16[64,512]{1,0:T(8,128)(2,1)S(1)} %fusion.15.teach_ref, bf16[1024,512]{1,0:T(8,128)(2,1)S(1)} %constant_dynamic-update-slice_fusion.3.capt_ref, s32[64,1]{1,0:T(8,128)S(1)} %copy.9.place_ref), custom_call_target="tpu_custom_call" | custom-call | tf_op jit(solution)/shard_map/loss_step/pallas_call | solution.py:99
  29.0 1.6 %collective-permute-start.15 = (bf16[264,128]{1,0:T(8,128)(2,1)S(1)}, bf16[264,128]{1,0:T(8,128)(2,1)S(1)}, u32[]{:S(2)}, u32[]{:S(2)}) collective-permute-start(bf16[264,128]{1,0:T(8,128)(2,1)S(1)} %loss_step.1), channel_id=1, source_target_pairs={{0,8},{4,12},{8,0},{12,4},{16,24},{20,28},{24,16},{28,20},{1,9},{5... | collective-permute-start | bytes 202760 | tf_op jit(solution)/shard_map/ppermute | solution.py:39
  30.6 1.3 %collective-permute-start.9 = (bf16[264,128]{1,0:T(8,128)(2,1)S(1)}, bf16[264,128]{1,0:T(8,128)(2,1)S(1)}, u32[]{:S(2)}, u32[]{:S(2)}) collective-permute-start(bf16[264,128]{1,0:T(8,128)(2,1)S(1)} %loss_step.1), channel_id=1, source_target_pairs={{0,16},{4,20},{8,24},{12,28},{16,0},{20,4},{24,8},{28,12},{1,17},{... | collective-permute-start | bytes 202760 | tf_op jit(solution)/shard_map/ppermute | solution.py:39
  31.9 1.6 %collective-permute-start.10 = (bf16[264,128]{1,0:T(8,128)(2,1)S(1)}, bf16[264,128]{1,0:T(8,128)(2,1)S(1)}, u32[]{:S(2)}, u32[]{:S(2)}) collective-permute-start(bf16[264,128]{1,0:T(8,128)(2,1)S(1)} %loss_step.1), channel_id=1, source_target_pairs={{0,24},{4,28},{8,16},{12,20},{16,8},{20,12},{24,0},{28,4},{1,25},{... | collective-permute-start | bytes 202760 | tf_op jit(solution)/shard_map/ppermute | solution.py:39
  33.5 1.6 %collective-permute-start.19 = (bf16[528,128]{1,0:T(8,128)(2,1)S(1)}, bf16[528,128]{1,0:T(8,128)(2,1)S(1)}, u32[]{:S(2)}, u32[]{:S(2)}) collective-permute-start(bf16[528,128]{1,0:T(8,128)(2,1)S(1)} %pad_maximum_fusion.5), channel_id=1, source_target_pairs={{0,4},{4,0},{8,12},{12,8},{16,20},{20,16},{24,28},{28,24},{1,5},{5... | collective-permute-start | bytes 405512 | tf_op jit(solution)/shard_map/ppermute | solution.py:39
  35.1 2.7 %collective-permute-done.17 = bf16[128,768]{1,0:T(8,128)(2,1)S(1)} collective-permute-done((bf16[128,768]{1,0:T(8,128)(2,1)S(1)}, bf16[128,768]{1,0:T(8,128)(2,1)S(1)}, u32[]{:S(2)}, u32[]{:S(2)}) %collective-permute-start.17) | collective-permute-done | bytes 196640 | tf_op jit(solution)/shard_map/ppermute | solution.py:39
  37.9 0.7 %collective-permute-done.9 = bf16[264,128]{1,0:T(8,128)(2,1)S(1)} collective-permute-done((bf16[264,128]{1,0:T(8,128)(2,1)S(1)}, bf16[264,128]{1,0:T(8,128)(2,1)S(1)}, u32[]{:S(2)}, u32[]{:S(2)}) %collective-permute-start.9) | collective-permute-done | bytes 67616 | tf_op jit(solution)/shard_map/ppermute | solution.py:39
  38.6 1.3 %collective-permute-start.11 = (bf16[528,128]{1,0:T(8,128)(2,1)S(1)}, bf16[528,128]{1,0:T(8,128)(2,1)S(1)}, u32[]{:S(2)}, u32[]{:S(2)}) collective-permute-start(bf16[528,128]{1,0:T(8,128)(2,1)S(1)} %pad_maximum_fusion.4), channel_id=1, source_target_pairs={{0,4},{4,0},{8,12},{12,8},{16,20},{20,16},{24,28},{28,24},{1,5},{5... | collective-permute-start | bytes 405512 | tf_op jit(solution)/shard_map/ppermute | solution.py:39
  40.0 0.3 convolution_bitcast_fusion.1
  40.3 0.3 convolution_bitcast_fusion.2
  40.8 3.3 %collective-permute-done.11.refs_0_ = bf16[528,128]{1,0:T(8,128)(2,1)S(1)} collective-permute-done((bf16[528,128]{1,0:T(8,128)(2,1)S(1)}, bf16[528,128]{1,0:T(8,128)(2,1)S(1)}, u32[]{:S(2)}, u32[]{:S(2)}) %collective-permute-start.11) | collective-permute-done | bytes 135200 | tf_op jit(solution)/shard_map/ppermute | solution.py:39
  44.0 0.4 convolution_bitcast_fusion
  44.4 1.2 %multiply_add_fusion = (f32[128,1024]{1,0:T(8,128)S(1)}, f32[128,1024]{1,0:T(8,128)S(1)}) fusion(f32[128,512]{1,0:T(8,128)S(1)} %convolution_bitcast_fusion, f32[128,256]{1,0:T(8,128)S(1)} %convolution_bitcast_fusion.1, f32[128,256]{1,0:T(8,128)S(1)} %convolution_bitcast_fusion.2), kind=kLoop, calls=%fused_computation.7 | loop fusion | flops 9175040 | bytes 1572864 | tf_op jit(solution)/shard_map/transpose(jvp())/add_any | solution.py:233
  45.7 0.9 %first_grads.1 = (f32[768,128]{1,0:T(8,128)S(1)}, f32[128,512]{1,0:T(8,128)S(1)}, f32[8,128]{1,0:T(8,128)S(1)}, bf16[768,256]{1,0:T(8,128)(2,1)S(1)}) custom-call(bf16[1584,128]{1,0:T(8,128)(2,1)S(1)} %constant_dynamic-update-slice_fusion.13.refs_0_, bf16[1584,128]{1,0:T(8,128)(2,1)S(1)} %collective-permute-done.20.refs_1_, ...), custom_call_target="tpu_custom_call" | custom-call | tf_op jit(solution)/shard_map/first_grads/pallas_call | solution.py:166
  46.6 1.4 %last_grads.1 = (f32[1,1]{1,0:T(1,128)}, f32[768,128]{1,0:T(8,128)}, f32[128,512]{1,0:T(8,128)}) custom-call(bf16[528,128]{1,0:T(8,128)(2,1)S(1)} %collective-permute-done.11.refs_0_, bf16[528,128]{1,0:T(8,128)(2,1)S(1)} %collective-permute-done.12.refs_1_, bf16[128,1024]{1,0:T(8,128)(2,1)S(1)} %multiply_convert_fusion.refs_5_.refs_2_, ...), custom_call_target="tpu_custom_call" | custom-call | tf_op jit(solution)/shard_map/last_grads/pallas_call | solution.py:204
  (72 shorter events, 2.0 us)
Async XLA Ops:
  0.6 4.1 %copy-start = (bf16[768,128]{1,0:T(8,128)(2,1)S(1)}, bf16[768,128]{1,0:T(8,128)(2,1)}, u32[]{:S(2)}) copy-start(bf16[768,128]{1,0:T(8,128)(2,1)} %param.9) | copy-start | bytes 589828
  0.6 7.7 %collective-permute-start.2 = (bf16[32,512]{1,0:T(8,128)(2,1)}, bf16[32,512]{1,0:T(8,128)(2,1)S(1)}, u32[]{:S(2)}, u32[]{:S(2)}) collective-permute-start(bf16[32,512]{1,0:T(8,128)(2,1)} %param.8), channel_id=1, source_target_pairs={{0,16},{4,20},{8,24},{12,28},{16,0},{20,4},{24,8},{28,12},{1,17},{... | collective-permute-start | bytes 98312 | tf_op jit(solution)/shard_map/ppermute | solution.py:39
  4.8 1.6 %copy-start.4 = (bf16[128,768]{1,0:T(8,128)(2,1)S(1)}, bf16[128,768]{1,0:T(8,128)(2,1)}, u32[]{:S(2)}) copy-start(bf16[128,768]{1,0:T(8,128)(2,1)} %param.6) | copy-start | bytes 589828
  4.8 3.3 %copy-start.2 = (bf16[128,512]{1,0:T(8,128)(2,1)S(1)}, bf16[128,512]{1,0:T(8,128)(2,1)}, u32[]{:S(2)}) copy-start(bf16[128,512]{1,0:T(8,128)(2,1)} %param.7) | copy-start | bytes 393220
  4.8 3.5 %copy-start.3 = (bf16[32,512]{1,0:T(8,128)(2,1)S(1)}, bf16[32,512]{1,0:T(8,128)(2,1)}, u32[]{:S(2)}) copy-start(bf16[32,512]{1,0:T(8,128)(2,1)} %param.8) | copy-start | bytes 98308
  6.3 11.2 %collective-permute-start = (f32[64,512]{1,0:T(8,128)S(1)}, f32[64,512]{1,0:T(8,128)S(1)}, u32[]{:S(2)}, u32[]{:S(2)}) collective-permute-start(f32[64,512]{1,0:T(8,128)S(1)} %constant_dynamic-slice_fusion.1), channel_id=1, source_target_pairs={{0,1},{1,0},{2,3},{3,2},{4,5},{5,4},{6,7},{7,6},{8,9},{9,8},{10,11... | collective-permute-start | bytes 393224 | tf_op jit(solution)/shard_map/ppermute | solution.py:39
  6.4 9.9 %collective-permute-start.13 = (bf16[64,768]{1,0:T(8,128)(2,1)S(1)}, bf16[64,768]{1,0:T(8,128)(2,1)S(1)}, u32[]{:S(2)}, u32[]{:S(2)}) collective-permute-start(bf16[64,768]{1,0:T(8,128)(2,1)S(1)} %constant_dynamic-slice_fusion), channel_id=1, source_target_pairs={{0,8},{4,12},{8,0},{12,4},{16,24},{20,28},{24,16},{28,20},{1,9},{5... | collective-permute-start | bytes 294920 | tf_op jit(solution)/shard_map/ppermute | solution.py:39
  8.3 4.7 %collective-permute-start.3 = (bf16[64,512]{1,0:T(8,128)(2,1)S(1)}, bf16[64,512]{1,0:T(8,128)(2,1)S(1)}, u32[]{:S(2)}, u32[]{:S(2)}) collective-permute-start(bf16[64,512]{1,0:T(8,128)(2,1)S(1)} %pad_maximum_fusion.6), channel_id=1, source_target_pairs={{0,8},{4,12},{8,0},{12,4},{16,24},{20,28},{24,16},{28,20},{1,9},{5... | collective-permute-start | bytes 196616 | tf_op jit(solution)/shard_map/ppermute | solution.py:39
  13.2 5.1 %collective-permute-start.4 = (bf16[128,512]{1,0:T(8,128)(2,1)S(1)}, bf16[128,512]{1,0:T(8,128)(2,1)S(1)}, u32[]{:S(2)}, u32[]{:S(2)}) collective-permute-start(bf16[128,512]{1,0:T(8,128)(2,1)S(1)} %constant_dynamic-update-slice_fusion), channel_id=1, source_target_pairs={{0,2},{1,3},{2,0},{3,1},{4,6},{5,7},{6,4},{7,5},{8,10},{9,11},{10,... | collective-permute-start | bytes 393224 | tf_op jit(solution)/shard_map/ppermute | solution.py:39
  14.7 5.0 %collective-permute-start.5 = (bf16[128,512]{1,0:T(8,128)(2,1)S(1)}, bf16[128,512]{1,0:T(8,128)(2,1)S(1)}, u32[]{:S(2)}, u32[]{:S(2)}) collective-permute-start(bf16[128,512]{1,0:T(8,128)(2,1)S(1)} %constant_dynamic-update-slice_fusion), channel_id=1, source_target_pairs={{0,4},{4,0},{8,12},{12,8},{16,20},{20,16},{24,28},{28,24},{1,5},{5... | collective-permute-start | bytes 393224 | tf_op jit(solution)/shard_map/ppermute | solution.py:39
  16.4 11.1 %collective-permute-start.14 = (bf16[128,768]{1,0:T(8,128)(2,1)S(1)}, bf16[128,768]{1,0:T(8,128)(2,1)S(1)}, u32[]{:S(2)}, u32[]{:S(2)}) collective-permute-start(bf16[128,768]{1,0:T(8,128)(2,1)S(1)} %pad_maximum_fusion.3), channel_id=1, source_target_pairs={{0,16},{4,20},{8,24},{12,28},{16,0},{20,4},{24,8},{28,12},{1,17},{... | collective-permute-start | bytes 589832 | tf_op jit(solution)/shard_map/ppermute | solution.py:39
  17.5 9.4 %collective-permute-start.1 = (f32[64,512]{1,0:T(8,128)S(1)}, f32[64,512]{1,0:T(8,128)S(1)}, u32[]{:S(2)}, u32[]{:S(2)}) collective-permute-start(f32[64,512]{1,0:T(8,128)S(1)} %dynamic-slice_add_fusion), channel_id=1, source_target_pairs={{0,2},{1,3},{2,0},{3,1},{4,6},{5,7},{6,4},{7,5},{8,10},{9,11},{10,... | collective-permute-start | bytes 393224 | tf_op jit(solution)/shard_map/ppermute | solution.py:39
  19.8 5.4 %collective-permute-start.6 = (bf16[128,512]{1,0:T(8,128)(2,1)S(1)}, bf16[128,512]{1,0:T(8,128)(2,1)S(1)}, u32[]{:S(2)}, u32[]{:S(2)}) collective-permute-start(bf16[128,512]{1,0:T(8,128)(2,1)S(1)} %collective-permute-done.5), channel_id=1, source_target_pairs={{0,2},{1,3},{2,0},{3,1},{4,6},{5,7},{6,4},{7,5},{8,10},{9,11},{10,... | collective-permute-start | bytes 393224 | tf_op jit(solution)/shard_map/ppermute | solution.py:39
  21.0 4.5 %copy-start.5 = (s32[128]{0:T(128)S(1)}, s32[128]{0:T(128)}, u32[]{:S(2)}) copy-start(s32[128]{0:T(128)} %param.11) | copy-start | bytes 1540
  21.0 4.6 %copy-start.1 = (bf16[128,512]{1,0:T(8,128)(2,1)S(1)}, bf16[128,512]{1,0:T(8,128)(2,1)}, u32[]{:S(2)}) copy-start(bf16[128,512]{1,0:T(8,128)(2,1)} %values_ref.1) | copy-start | bytes 393220
  21.3 6.7 %collective-permute-start.7 = (bf16[384,512]{1,0:T(8,128)(2,1)S(1)}, bf16[384,512]{1,0:T(8,128)(2,1)S(1)}, u32[]{:S(2)}, u32[]{:S(2)}) collective-permute-start(bf16[384,512]{1,0:T(8,128)(2,1)S(1)} %pad_maximum_fusion.2), channel_id=1, source_target_pairs={{0,1},{1,0},{2,3},{3,2},{4,5},{5,4},{6,7},{7,6},{8,9},{9,8},{10,11... | collective-permute-start | bytes 1179656 | tf_op jit(solution)/shard_map/ppermute | solution.py:39
  25.4 2.6 %collective-permute-start.8 = (bf16[128,512]{1,0:T(8,128)(2,1)S(1)}, bf16[128,512]{1,0:T(8,128)(2,1)S(1)}, u32[]{:S(2)}, u32[]{:S(2)}) collective-permute-start(bf16[128,512]{1,0:T(8,128)(2,1)S(1)} %get-tuple-element.28), channel_id=1, source_target_pairs={{0,1},{1,0},{2,3},{3,2},{4,5},{5,4},{6,7},{7,6},{8,9},{9,8},{10,11... | collective-permute-start | bytes 393224 | tf_op jit(solution)/shard_map/ppermute | solution.py:39
  25.8 9.3 %collective-permute-start.16 = (bf16[128,768]{1,0:T(8,128)(2,1)S(1)}, bf16[128,768]{1,0:T(8,128)(2,1)S(1)}, u32[]{:S(2)}, u32[]{:S(2)}) collective-permute-start(bf16[128,768]{1,0:T(8,128)(2,1)S(1)} %pad_maximum_fusion.3), channel_id=1, source_target_pairs={{0,4},{4,0},{8,12},{12,8},{16,20},{20,16},{24,28},{28,24},{1,5},{5... | collective-permute-start | bytes 589832 | tf_op jit(solution)/shard_map/ppermute | solution.py:39
  27.5 10.3 %collective-permute-start.17 = (bf16[128,768]{1,0:T(8,128)(2,1)S(1)}, bf16[128,768]{1,0:T(8,128)(2,1)S(1)}, u32[]{:S(2)}, u32[]{:S(2)}) collective-permute-start(bf16[128,768]{1,0:T(8,128)(2,1)S(1)} %collective-permute-done.14), channel_id=1, source_target_pairs={{0,4},{4,0},{8,12},{12,8},{16,20},{20,16},{24,28},{28,24},{1,5},{5... | collective-permute-start | bytes 589832 | tf_op jit(solution)/shard_map/ppermute | solution.py:39
  29.0 4.5 %collective-permute-start.15 = (bf16[264,128]{1,0:T(8,128)(2,1)S(1)}, bf16[264,128]{1,0:T(8,128)(2,1)S(1)}, u32[]{:S(2)}, u32[]{:S(2)}) collective-permute-start(bf16[264,128]{1,0:T(8,128)(2,1)S(1)} %loss_step.1), channel_id=1, source_target_pairs={{0,8},{4,12},{8,0},{12,4},{16,24},{20,28},{24,16},{28,20},{1,9},{5... | collective-permute-start | bytes 202760 | tf_op jit(solution)/shard_map/ppermute | solution.py:39
  30.6 8.1 %collective-permute-start.9 = (bf16[264,128]{1,0:T(8,128)(2,1)S(1)}, bf16[264,128]{1,0:T(8,128)(2,1)S(1)}, u32[]{:S(2)}, u32[]{:S(2)}) collective-permute-start(bf16[264,128]{1,0:T(8,128)(2,1)S(1)} %loss_step.1), channel_id=1, source_target_pairs={{0,16},{4,20},{8,24},{12,28},{16,0},{20,4},{24,8},{28,12},{1,17},{... | collective-permute-start | bytes 202760 | tf_op jit(solution)/shard_map/ppermute | solution.py:39
  31.9 6.8 %collective-permute-start.10 = (bf16[264,128]{1,0:T(8,128)(2,1)S(1)}, bf16[264,128]{1,0:T(8,128)(2,1)S(1)}, u32[]{:S(2)}, u32[]{:S(2)}) collective-permute-start(bf16[264,128]{1,0:T(8,128)(2,1)S(1)} %loss_step.1), channel_id=1, source_target_pairs={{0,24},{4,28},{8,16},{12,20},{16,8},{20,12},{24,0},{28,4},{1,25},{... | collective-permute-start | bytes 202760 | tf_op jit(solution)/shard_map/ppermute | solution.py:39
  33.5 7.1 %collective-permute-start.19 = (bf16[528,128]{1,0:T(8,128)(2,1)S(1)}, bf16[528,128]{1,0:T(8,128)(2,1)S(1)}, u32[]{:S(2)}, u32[]{:S(2)}) collective-permute-start(bf16[528,128]{1,0:T(8,128)(2,1)S(1)} %pad_maximum_fusion.5), channel_id=1, source_target_pairs={{0,4},{4,0},{8,12},{12,8},{16,20},{20,16},{24,28},{28,24},{1,5},{5... | collective-permute-start | bytes 405512 | tf_op jit(solution)/shard_map/ppermute | solution.py:39
  37.8 6.2 %collective-permute-start.18 = (bf16[512,768]{1,0:T(8,128)(2,1)S(1)}, bf16[512,768]{1,0:T(8,128)(2,1)S(1)}, u32[]{:S(2)}, u32[]{:S(2)}) collective-permute-start(bf16[512,768]{1,0:T(8,128)(2,1)S(1)} %pad_maximum_fusion), channel_id=1, source_target_pairs={{0,1},{1,0},{2,3},{3,2},{4,5},{5,4},{6,7},{7,6},{8,9},{9,8},{10,11... | collective-permute-start | bytes 2359304 | tf_op jit(solution)/shard_map/ppermute | solution.py:39
  38.6 5.4 %collective-permute-start.11 = (bf16[528,128]{1,0:T(8,128)(2,1)S(1)}, bf16[528,128]{1,0:T(8,128)(2,1)S(1)}, u32[]{:S(2)}, u32[]{:S(2)}) collective-permute-start(bf16[528,128]{1,0:T(8,128)(2,1)S(1)} %pad_maximum_fusion.4), channel_id=1, source_target_pairs={{0,4},{4,0},{8,12},{12,8},{16,20},{20,16},{24,28},{28,24},{1,5},{5... | collective-permute-start | bytes 405512 | tf_op jit(solution)/shard_map/ppermute | solution.py:39
  40.7 5.0 %collective-permute-start.20 = (bf16[1584,128]{1,0:T(8,128)(2,1)S(1)}, bf16[1584,128]{1,0:T(8,128)(2,1)S(1)}, u32[]{:S(2)}, u32[]{:S(2)}) collective-permute-start(bf16[1584,128]{1,0:T(8,128)(2,1)S(1)} %constant_dynamic-update-slice_fusion.13.refs_0_), channel_id=1, source_target_pairs={{0,1},{1,0},{2,3},{3,2},{4,5},{5,4},{6,7},{7,6},{8,9},{9,8},{10,11... | collective-permute-start | bytes 1216520 | tf_op jit(solution)/shard_map/ppermute | solution.py:39
  44.0 2.6 %collective-permute-start.12 = (bf16[528,128]{1,0:T(8,128)(2,1)S(1)}, bf16[528,128]{1,0:T(8,128)(2,1)S(1)}, u32[]{:S(2)}, u32[]{:S(2)}) collective-permute-start(bf16[528,128]{1,0:T(8,128)(2,1)S(1)} %collective-permute-done.11.refs_0_), channel_id=1, source_target_pairs={{0,1},{1,0},{2,3},{3,2},{4,5},{5,4},{6,7},{7,6},{8,9},{9,8},{10,11... | collective-permute-start | bytes 405512 | tf_op jit(solution)/shard_map/ppermute | solution.py:39
